TPU v7x, 32 devices: a whole 2x2x4 slice. The times are simulated.
32 devices in a mesh: section: 8 (over y, x, core), dp: 4 (over z).
Axes of the slice: x: 2, y: 2, z: 4, core: 2. Of those that a mesh axis runs over, the one named last changes fastest.
Arguments:
- activations: bfloat16 [2048, 8192], P('dp'), may hold values from -6 to 6
- cotangent: bfloat16 [2048, 8192], P('dp'), may hold values from -6 to 6
- gate_pre: bfloat16 [2048, 4096], P('dp', 'section'), may hold values from -6 to 6
- weights: bfloat16 [2, 8192, 4096], P(None, 'dp', 'section'), may hold values from -0.0625 to 0.0625
- holder_map: int32 [64, 8, 2], P('dp', 'section'), may hold values from 0 to 7, as said below
- master: float32 [8, 4, 48, 128, 512], P('section', 'dp'), may hold values from -0.0625 to 0.0625
- moment_one: float32 [8, 4, 48, 128, 512], P('section', 'dp'), may hold values from -80 to 80
- moment_two: float32 [8, 4, 48, 128, 512], P('section', 'dp'), may hold values from 102.4 to 4096
- adam_step: int32 [1], replicated, may hold values from 1 to 11
Outputs:
- passed_back: bfloat16 [2048, 8192], P('dp', 'section')
- new_weights: bfloat16 [2, 8192, 4096], P(None, 'dp', 'section')
Inputs may be any that keep to these rules, and one draw needn't show every extreme that they name: `holder_map`: every block of one device (32 of them) goes to holders of that device's dp index; one device sends to exactly 4 holder sections, exactly 8 blocks to each; each holder device receives at most 48 blocks from all sections, and in every dp column some holder receives exactly 48.
All inputs are finite; a program needn't handle non-finite values.
Results may differ from a plain program's by a relative error of at most 0.012.
Values may be sent and summed in bfloat16 or wider, within the bound.
A program may use at most 320 MiB of HBM per device.

v0:
```python
import jax
import jax.numpy as jnp
from jax import lax
from jax.sharding import PartitionSpec as P

learn_rate = 0.03
beta_one = 0.9
beta_two = 0.95
adam_eps = 1e-08
decay_rate = 0.1


def carried_in(shard, axis, combine, identity):
    devices, position = (lax.axis_size(axis), lax.axis_index(axis))
    everything = lax.all_gather(shard, axis)
    start = jnp.broadcast_to(jnp.asarray(identity, shard.dtype), shard.shape)

    def hop(k, before):
        reached = k < position
        new = combine(before, everything[k])
        return jnp.where(reached, new, before)

    return lax.fori_loop(0, devices, hop, start)


def adam_apply(gradient, weight_master, first_moment, second_moment, step_number):
    step_float = step_number.astype(jnp.float32)
    fix_one = 1.0 - jnp.power(jnp.float32(beta_one), step_float)
    fix_two = 1.0 - jnp.power(jnp.float32(beta_two), step_float)
    first_new = beta_one * first_moment + (1.0 - beta_one) * gradient
    second_new = beta_two * second_moment + (1.0 - beta_two) * gradient * gradient
    update = first_new / fix_one / (jnp.sqrt(second_new / fix_two) + adam_eps)
    return (weight_master * (1.0 - learn_rate * decay_rate) - learn_rate * update).astype(
        jnp.bfloat16
    )


def per_device(
    activations, cotangent, gate_pre, weights, holder_map, master, moment_one, moment_two, adam_step
):
    hidden_units = gate_pre.shape[1]
    row_count = weights.shape[1]
    sections = lax.axis_size("section")
    contract = (((1,), (1,)), ((), ()))
    over_tokens = (((0,), (0,)), ((), ()))
    gathered = lax.all_gather(weights, "dp", axis=1, tiled=True)
    up_full = gathered[0]
    lifted = jnp.dot(activations, up_full, preferred_element_type=jnp.float32)
    back_hidden = jnp.dot(cotangent, gathered[1], preferred_element_type=jnp.float32)
    gate_silu = jax.nn.silu(gate_pre.astype(jnp.float32))
    hidden = (gate_silu * lifted).astype(jnp.bfloat16)
    back_up = (back_hidden * gate_silu).astype(jnp.bfloat16)
    back_in = lax.dot_general(back_up, up_full, contract, preferred_element_type=jnp.float32)
    passed_back = lax.psum_scatter(
        back_in.astype(jnp.bfloat16), "section", scatter_dimension=1, tiled=True
    )
    summed = lax.psum_scatter(
        jnp.concatenate(
            [
                lax.dot_general(
                    activations, back_up, over_tokens, preferred_element_type=jnp.float32
                ),
                lax.dot_general(cotangent, hidden, over_tokens, preferred_element_type=jnp.float32),
            ],
            axis=1,
        ).astype(jnp.bfloat16),
        "dp",
        scatter_dimension=0,
        tiled=True,
    ).astype(jnp.float32)
    block_rows = master.shape[3]
    capacity = master.shape[2]
    row_blocks = row_count // block_rows
    per_dest = 4 * row_blocks // sections
    blocks = (
        summed.reshape(row_blocks, block_rows, 2, hidden_units)
        .transpose(0, 2, 1, 3)
        .reshape(-1, block_rows, hidden_units)
    )
    block_total = blocks.shape[0]
    owners = holder_map[:, 0, :].reshape(-1)
    section_ids = jnp.arange(sections, dtype=jnp.int32)
    choose = (owners[:, None] == section_ids[None, :]).astype(jnp.int32)
    ahead = jnp.cumsum(choose, axis=0) - choose
    order_in = jnp.sum(ahead * choose, axis=1)
    totals = jnp.sum(choose, axis=0)
    earlier = carried_in(
        totals,
        "section",
        lambda first_part, later_part: first_part + later_part,
        jnp.zeros_like(totals),
    )
    slot_of = order_in + jnp.sum(choose * earlier[None, :], axis=1).astype(jnp.int32)
    chosen = (owners[None, None, :] == section_ids[:, None, None]) & (
        order_in[None, None, :] == jnp.arange(per_dest, dtype=jnp.int32)[None, :, None]
    )
    present = jnp.any(chosen, axis=2)
    source_index = jnp.sum(
        jnp.where(chosen, jnp.arange(block_total, dtype=jnp.int32)[None, None, :], 0), axis=2
    )
    outgoing = jnp.take(blocks, source_index.reshape(-1), axis=0).reshape(
        sections, per_dest, block_rows, hidden_units
    )
    out_slot = jnp.where(
        present, jnp.sum(jnp.where(chosen, slot_of[None, None, :], 0), axis=2), capacity
    )
    step_number = adam_step[0]
    states = (master[0, 0], moment_one[0, 0], moment_two[0, 0])
    arrivals = lax.all_to_all(
        outgoing.astype(jnp.bfloat16), "section", split_axis=0, concat_axis=0, tiled=True
    ).astype(outgoing.dtype)
    item_slots = lax.all_to_all(out_slot, "section", split_axis=0, concat_axis=0, tiled=True)
    live = (item_slots < capacity).astype(jnp.float32).reshape(item_slots.shape + (1, 1))
    slot_index = jnp.minimum(item_slots, capacity - 1).reshape(-1)
    looked = [jnp.take(state, slot_index, axis=0).reshape(arrivals.shape) for state in states]
    updated = adam_apply(
        arrivals * live,
        looked[0] * live,
        looked[1] * live,
        looked[2] * live + (1.0 - live),
        step_number,
    )
    returned = lax.all_to_all(updated, "section", split_axis=0, concat_axis=0, tiled=True)
    new_blocks = jnp.take(
        returned.reshape(-1, block_rows, hidden_units), owners * per_dest + order_in, axis=0
    )
    new_rows = (
        new_blocks.reshape(row_blocks, 2, block_rows, hidden_units)
        .transpose(1, 0, 2, 3)
        .reshape(2, row_count, hidden_units)
    )
    return (passed_back, new_rows)


def solution(mesh):
    in_specs = (
        P("dp", None),
        P("dp", None),
        P("dp", "section"),
        P(None, "dp", "section"),
        P("dp", "section", None),
        P("section", "dp", None, None, None),
        P("section", "dp", None, None, None),
        P("section", "dp", None, None, None),
        P(),
    )
    out_specs = (P("dp", "section"), P(None, "dp", "section"))
    return jax.shard_map(
        per_device, mesh=mesh, in_specs=in_specs, out_specs=out_specs, check_vma=False
    )
```

profile of v0, /device:TPU:0, one launch (start us, length us, event | category | flops | bytes accessed | tf_op | source)
XLA Modules:
  0.0 910.2 jit_solution(6311418935512518231)
XLA Ops:
  7.2 0.7 all-gather.3.cloned.1.call-update
  7.9 291.1 %all-gather.3.cloned.1.call-done = bf16[2,8192,512]{2,1,0:T(8,128)(2,1)} async-done(((bf16[2,2048,512]{2,1,0:T(8,128)(2,1)}), bf16[2,8192,512]{2,1,0:T(8,128)(2,1)}) %all-gather.3.cloned.1.call-update) | async-done | bytes 16777232 | tf_op jit(solution)/shard_map/all_gather | solution.py:46
  299.1 10.4 %fusion.12 = bf16[512,512]{1,0:T(8,128)(2,1)S(1)} fusion(bf16[512,8192]{1,0:T(8,128)(2,1)} %param.14, bf16[2,8192,512]{2,1,0:T(8,128)(2,1)} %all-gather.3.cloned.1.call-done, bf16[512,512]{1,0:T(8,128)(2,1)} %param.15), kind=kOutput, calls=%fused_computation.35 | convolution fusion | flops 4296802304 | bytes 17825792 | tf_op jit(solution)/shard_map/dot_general | solution.py:49
  309.5 8.3 fusion.6
  317.8 7.1 fusion.13
  325.0 8.2 fusion.7
  333.2 6.7 pad_maximum_fusion
  339.9 0.6 copy-done.1
  340.5 0.1 copy.33
  340.6 0.1 reshape_squeeze.3
  340.7 0.6 dynamic-slice
  341.9 0.1 fusion.20
  342.0 0.2 dynamic-update-slice
  342.3 7.9 all-reduce
  350.2 0.1 reshape.271
  350.3 0.1 fusion.19
  350.4 0.3 while.14
  350.7 0.2 select_reduce_fusion
  351.0 0.2 and_reduce_fusion
  351.2 0.4 fusion.18
  351.6 0.6 broadcast_select_fusion.5
  352.2 3.5 all-to-all-start
  355.7 0.1 reshape.221
  355.8 262.8 %reduce-scatter.5.cloned.1.call-done = bf16[2048,1024]{0,1:T(8,128)(2,1)} async-done(((bf16[8192,1024]{0,1:T(8,128)(2,1)}), bf16[2048,1024]{0,1:T(8,128)(2,1)}) %reduce-scatter.5.cloned.1.call-update) | async-done | bytes 4194320 | tf_op jit(solution)/shard_map/reduce_scatter | solution.py:57
  618.6 5.6 copy.41
  624.2 7.6 copy.38
  631.8 7.6 gather_fusion
  639.4 10.4 %select_convert_fusion = bf16[8,8,128,512]{3,2,1,0:T(8,128)(2,1)} fusion(bf16[8,8,128,512]{3,2,1,0:T(8,128)(2,1)} %bitcast.83, pred[8,8]{1,0:T(8,128)(4,1)S(1)} %compare_and_fusion), kind=kLoop, calls=%fused_computation.16 | loop fusion | flops 4194304 | bytes 16777280 | tf_op jit(solution)/shard_map/convert_element_type | solution.py:110
  649.8 4.9 all-to-all-start.1
  654.8 0.3 reduce-scatter.3.cloned.1.call-start
  655.8 0.1 min.12
  655.9 13.0 %gather_fusion.4 = f32[64,128,512]{2,1,0:T(8,128)} fusion(f32[48,128,512]{2,1,0:T(8,128)} %bitcast.84, s32[1024]{0:T(1024)S(1)} %pad_clamp_fusion.2), kind=kCustom, calls=%fused_computation.2.clone | custom fusion | bytes 33554688 | tf_op jit(solution)/shard_map/jit(_take)/gather | solution.py:115
  668.8 13.0 %gather_fusion.3 = f32[64,128,512]{2,1,0:T(8,128)} fusion(f32[48,128,512]{2,1,0:T(8,128)} %bitcast.85, s32[1024]{0:T(1024)S(1)} %pad_clamp_fusion.2), kind=kCustom, calls=%fused_computation.1.clone | custom fusion | bytes 33554688 | tf_op jit(solution)/shard_map/jit(_take)/gather | solution.py:115
  681.8 12.9 %gather_fusion.2 = f32[64,128,512]{2,1,0:T(8,128)} fusion(f32[48,128,512]{2,1,0:T(8,128)} %bitcast.86, s32[1024]{0:T(1024)S(1)} %pad_clamp_fusion.2), kind=kCustom, calls=%fused_computation.clone | custom fusion | bytes 33554688 | tf_op jit(solution)/shard_map/jit(_take)/gather | solution.py:115
  694.8 33.9 %broadcast_select_fusion.3 = (f32[64,128,512]{2,1,0:T(8,128)}, f32[64,128,512]{2,1,0:T(8,128)}, f32[64,128,512]{2,1,0:T(8,128)}) fusion(f32[64,128,512]{2,1,0:T(8,128)} %gather_fusion.3, pred[64]{0:T(512)(128)(4,1)S(1)} %compare_and_fusion.1, f32[64,128,512]{2,1,0:T(8,128)} %gather_fusion.4, f32[64,128,512]{2,1,0:T(8,128)} %gather_fusion.2), kind=kLoop, calls=%fused_computation.26 | loop fusion | flops 12582912 | bytes 100663360 | tf_op jit(solution)/shard_map/jit(_take)/select_n | solution.py:115
  728.6 10.1 %convolution_convert_fusion.2 = bf16[512,8192]{1,0:T(8,128)(2,1)} fusion(bf16[512,512]{1,0:T(8,128)(2,1)S(1)} %fusion.12, bf16[2,8192,512]{2,1,0:T(8,128)(2,1)} %all-gather.3.cloned.1.call-done), kind=kOutput, calls=%fused_computation.19 | convolution fusion | flops 4299161600 | bytes 17301504 | tf_op jit(solution)/shard_map/dot_general | solution.py:53
  738.7 10.1 %all-to-all-done.1 = bf16[8,8,128,512]{3,2,1,0:T(8,128)(2,1)} async-done(((bf16[8,8,128,512]{3,2,1,0:T(8,128)(2,1)}), bf16[8,8,128,512]{3,2,1,0:T(8,128)(2,1)}, u32[]{:S(2)}, u32[]{:S(2)}) %all-to-all-start.1) | async-done | bytes 8388640 | tf_op jit(solution)/shard_map/all_to_all | solution.py:109
  748.8 28.3 %subtract_convert_fusion = bf16[8,8,128,512]{3,2,1,0:T(8,128)(2,1)} fusion(f32[8,8,128,512]{3,2,1,0:T(8,128)} %bitcast.81, f32[8,8,128,512]{3,2,1,0:T(8,128)} %bitcast.80, bf16[8,8,128,512]{3,2,1,0:T(8,128)(2,1)} %all-to-all-done.1, f32[8,8,128,512]{3,2,1,0:T(8,128)} %bitcast.79, f32[]{:T(128)} %bitcast.21, f32[8,8]{1,0:T(8,128)S(1)} %broadcast_subtract_fusion, ...), kind=kLoop, calls=%fused_computation.15 | loop fusion | flops 88080384 | bytes 67109384 | tf_op jit(solution)/shard_map/convert_element_type | solution.py:33
  777.1 5.0 all-to-all-start.2
  782.1 0.1 reduce_sum.50
  782.2 0.1 copy.39
  782.2 0.1 mul.135
  782.3 0.1 copy.34
  782.4 0.1 copy.35
  782.6 109.7 %all-to-all-done.2 = bf16[8,8,128,512]{3,2,1,0:T(8,128)(2,1)} async-done(((bf16[8,8,128,512]{3,2,1,0:T(8,128)(2,1)}), bf16[8,8,128,512]{3,2,1,0:T(8,128)(2,1)}, u32[]{:S(2)}, u32[]{:S(2)}) %all-to-all-start.2) | async-done | bytes 8388640 | tf_op jit(solution)/shard_map/all_to_all | solution.py:123
  892.3 6.2 gather_fusion.1
  898.5 2.6 select_bitcast_fusion
  901.1 2.5 copy.40
  (40 shorter events, 0.4 us)
Async XLA Ops:
  7.2 291.9 %all-gather.3.cloned.1.call-start = ((), (), s32[]{:S(2)}) async-start(), calls=%async_computation.5 | async-start | bytes 20971520 | tf_op jit(solution)/shard_map/all_gather | solution.py:46
  7.9 610.7 %reduce-scatter.5.cloned.1.call-start = ((), (), s32[]{:S(2)}) async-start(), calls=%async_computation.7 | async-start | bytes 20971520 | tf_op jit(solution)/shard_map/reduce_scatter | solution.py:57
  309.5 8.4 copy-start
  309.5 8.4 copy-start.2
  339.9 0.7 copy-start.1
  339.9 0.9 copy-start.3
  352.2 297.6 %all-to-all-start = ((s32[8,1,8]{2,1,0:T(1,128)}), s32[8,1,8]{2,1,0:T(1,128)S(1)}, u32[]{:S(2)}, u32[]{:S(2)}) async-start(s32[8,1,8]{2,1,0:T(1,128)} %bitcast.5), calls=%async_computation.1 | async-start | bytes 8192 | tf_op jit(solution)/shard_map/all_to_all | solution.py:112
  649.8 99.0 %all-to-all-start.1 = ((bf16[8,8,128,512]{3,2,1,0:T(8,128)(2,1)}), bf16[8,8,128,512]{3,2,1,0:T(8,128)(2,1)}, u32[]{:S(2)}, u32[]{:S(2)}) async-start(bf16[8,8,128,512]{3,2,1,0:T(8,128)(2,1)} %select_convert_fusion), calls=%async_computation.3 | async-start | bytes 16777216 | tf_op jit(solution)/shard_map/all_to_all | solution.py:109
  654.8 248.9 %reduce-scatter.3.cloned.1.call-start = ((), (), s32[]{:S(2)}) async-start(), calls=%async_computation.6 | async-start | bytes 9437184 | tf_op jit(solution)/shard_map/reduce_scatter | solution.py:54
  777.1 115.2 %all-to-all-start.2 = ((bf16[8,8,128,512]{3,2,1,0:T(8,128)(2,1)}), bf16[8,8,128,512]{3,2,1,0:T(8,128)(2,1)}, u32[]{:S(2)}, u32[]{:S(2)}) async-start(bf16[8,8,128,512]{3,2,1,0:T(8,128)(2,1)} %subtract_convert_fusion), calls=%async_computation.4 | async-start | bytes 16777216 | tf_op jit(solution)/shard_map/all_to_all | solution.py:123
Sparse Core Ops, SparseCore 0:
  9.6 289.4 all-gather.2
  340.0 278.5 reduce-scatter.4
  738.9 121.1 reduce-scatter.2
where the time goes:
time: 911 us; the launch traced here: 910 us
  waiting for transfers between devices  674 us (74%)
  other arithmetic  83.7 us (9%)
  local copies, waits for them, and re-layouts  70.7 us (8%)
  matrix products  44.1 us (5%)
  between operations  15.3 us (2%)
  starting transfers between devices  13.7 us (2%)
    all_gather x1, waiting for transfers between devices, per_device(): gathered = lax.all_gather(weights, 'dp', axis=1, tiled=True)  291 us
    reduce_scatter x1, waiting for transfers between devices, per_device(): lax.psum_scatter(jnp.concatenate([lax.dot_general(activations, back_up, o...  263 us
    all_to_all x1, waiting for transfers between devices, per_device(): lax.all_to_all(updated, 'section', split_axis=0, concat_axis=0, tiled=True)  110 us
    gather x3, local copies, waits for them, and re-layouts, per_device(): jnp.take(state, slot_index, axis=0).reshape(arrivals.shape)  38.9 us
    select_n x2, other arithmetic, per_device(): jnp.take(state, slot_index, axis=0).reshape(arrivals.shape)  33.9 us
    convert_element_type x1, other arithmetic, adam_apply(): (weight_master * (1.0 - learn_rate * decay_rate) - learn_rate * update).a...  28.3 us
  transfers between devices with their start and end apart: 6, of which 4 were waited for; matrix products, arithmetic and copies ran while one was open for 17% of the time, Pallas kernels for 0%

commit v1 on v0

v1 whole, which is shorter than its diff:
```python
import jax
import jax.numpy as jnp
from jax import lax
from jax.experimental import pallas as pl
from jax.experimental.pallas import tpu as pltpu
from jax.sharding import PartitionSpec as P

learn_rate = 0.03
beta_one = 0.9
beta_two = 0.95
adam_eps = 1e-08
decay_rate = 0.1

BF16 = jnp.bfloat16
F32 = jnp.float32


def adam_kernel(item_ref, count_ref, fix_ref, grad_ref, w_ref, a_ref, b_ref, out_ref):
    @pl.when(pl.program_id(0) < count_ref[0])
    def _():
        grad = grad_ref[0].astype(F32)
        first = beta_one * a_ref[0] + (1.0 - beta_one) * grad
        second = beta_two * b_ref[0] + (1.0 - beta_two) * grad * grad
        update = first / fix_ref[0] / (jnp.sqrt(second / fix_ref[1]) + adam_eps)
        out_ref[0] = (
            w_ref[0] * (1.0 - learn_rate * decay_rate) - learn_rate * update
        ).astype(BF16)


def adam_slots(items, count, fixes, arrivals, states, chunk):
    total, rows, cols = arrivals.shape
    capacity = states[0].shape[0]

    def at_slot(c, item_ref, count_ref):
        return (jnp.minimum(c, jnp.maximum(count_ref[0] - 1, 0)), 0, chunk)

    def at_item(c, item_ref, count_ref):
        return (item_ref[c], 0, 0)

    state_spec = pl.BlockSpec((1, rows, cols), at_slot)
    item_spec = pl.BlockSpec((1, rows, cols), at_item)
    return pl.pallas_call(
        adam_kernel,
        out_shape=jax.ShapeDtypeStruct(arrivals.shape, BF16),
        grid_spec=pltpu.PrefetchScalarGridSpec(
            num_scalar_prefetch=2,
            grid=(capacity,),
            in_specs=[pl.BlockSpec(memory_space=pltpu.SMEM), item_spec] + [state_spec] * 3,
            out_specs=item_spec,
        ),
        cost_estimate=pl.CostEstimate(
            flops=20 * capacity * rows * cols,
            bytes_accessed=16 * capacity * rows * cols,
            transcendentals=capacity * rows * cols,
        ),
        name="adam",
    )(items, count, fixes, arrivals, *states)


def move_kernel(index_ref, in_ref, out_ref):
    out_ref[...] = in_ref[...].reshape(out_ref.shape)


def pick_rows(index, table, rows, matrices_first):
    count = index.shape[0]
    cols = table.shape[2]
    return pl.pallas_call(
        move_kernel,
        out_shape=jax.ShapeDtypeStruct((count, rows, cols), table.dtype),
        grid_spec=pltpu.PrefetchScalarGridSpec(
            num_scalar_prefetch=1,
            grid=(count,),
            in_specs=[pl.BlockSpec((1, rows, cols), lambda i, ix: (ix[i] % 2, ix[i] // 2, 0))],
            out_specs=pl.BlockSpec((1, rows, cols), lambda i, ix: (i, 0, 0)),
        ),
        name="pick_rows",
    )(index, table)


def place_rows(index, parts, row_blocks):
    rows, cols = parts[0].shape[1:]
    width = cols * len(parts)

    def body(index_ref, *refs):
        out_ref = refs[-1]
        for at, ref in enumerate(refs[:-1]):
            out_ref[0, :, at * cols : (at + 1) * cols] = ref[0]

    return pl.pallas_call(
        body,
        out_shape=jax.ShapeDtypeStruct((2, row_blocks * rows, width), parts[0].dtype),
        grid_spec=pltpu.PrefetchScalarGridSpec(
            num_scalar_prefetch=1,
            grid=(row_blocks * 2,),
            in_specs=[pl.BlockSpec((1, rows, cols), lambda i, ix: (ix[i], 0, 0))] * len(parts),
            out_specs=pl.BlockSpec((1, rows, width), lambda i, ix: (i % 2, i // 2, 0)),
        ),
        name="place_rows",
    )(index, *parts)


def per_device(
    activations, cotangent, gate_pre, weights, holder_map, master, moment_one, moment_two, adam_step
):
    sections = lax.axis_size("section")
    ranks = lax.axis_size("dp")
    here = lax.axis_index("section")
    tok_dev, width = activations.shape
    piece = tok_dev // sections
    row_count, hidden_units = weights.shape[1:]
    block_rows = master.shape[3]
    capacity = master.shape[2]
    row_blocks = row_count // block_rows
    per_dest = 4 * row_blocks // sections
    over_tokens = (((0,), (0,)), ((), ()))

    owners = holder_map[:, 0, :].reshape(-1)
    section_ids = jnp.arange(sections, dtype=jnp.int32)
    choose = (owners[:, None] == section_ids[None, :]).astype(jnp.int32)
    order_in = jnp.sum((jnp.cumsum(choose, axis=0) - choose) * choose, axis=1)
    totals = jnp.sum(choose, axis=0)
    every_total = lax.all_gather(totals, "section")
    place = owners * per_dest + order_in
    wanted = jnp.arange(sections * per_dest, dtype=jnp.int32)
    source = jnp.sum(
        jnp.where(
            place[None, :] == wanted[:, None],
            jnp.arange(place.shape[0], dtype=jnp.int32)[None, :],
            0,
        ),
        axis=1,
    )
    mine = jnp.sum(jnp.where(section_ids[None, :] == here, every_total, 0), axis=1)
    before = jnp.cumsum(mine) - mine
    count = jnp.sum(mine)
    spot = jnp.arange(per_dest, dtype=jnp.int32)
    slot = jnp.where(spot[None, :] < mine[:, None], before[:, None] + spot[None, :], -1).reshape(-1)
    slots = jnp.minimum(jnp.arange(capacity, dtype=jnp.int32), jnp.maximum(count - 1, 0))
    items = jnp.sum(jnp.where(slot[None, :] == slots[:, None], wanted[None, :], 0), axis=1)
    step_float = adam_step[0].astype(F32)
    fixes = jnp.stack(
        [
            1.0 - jnp.power(jnp.float32(beta_one), step_float),
            1.0 - jnp.power(jnp.float32(beta_two), step_float),
        ]
    )

    def spread(tokens):
        own = lax.dynamic_slice_in_dim(tokens, here * piece, piece, 0)
        swapped = lax.all_to_all(own, "dp", split_axis=1, concat_axis=0, tiled=True)
        return lax.all_gather(swapped, "section", axis=0, tiled=True)

    def project(full, matrix):
        part = jnp.dot(full, matrix, preferred_element_type=F32).astype(BF16)
        part = part.reshape(sections, ranks, piece, hidden_units).transpose(1, 0, 2, 3)
        part = part.reshape(ranks * tok_dev, hidden_units)
        return lax.psum_scatter(part, "dp", scatter_dimension=0, tiled=True).astype(F32)

    def all_tokens(local):
        out = lax.all_gather(local, "dp", axis=0, tiled=True)
        out = out.reshape(ranks, sections, piece, hidden_units).transpose(1, 0, 2, 3)
        return out.reshape(ranks * tok_dev, hidden_units)

    cot_full = spread(cotangent)
    act_full = spread(activations)
    back_hidden = project(cot_full, weights[1])
    lifted = project(act_full, weights[0])
    gate_silu = jax.nn.silu(gate_pre.astype(F32))
    back_up = all_tokens((back_hidden * gate_silu).astype(BF16))
    hidden = all_tokens((gate_silu * lifted).astype(BF16))

    split = sections // ranks
    in_part = lax.dot_general(
        back_up, weights[0], (((1,), (1,)), ((), ())), preferred_element_type=F32
    ).astype(BF16)
    in_part = in_part.reshape(sections, ranks, piece, split, row_count // split)
    in_part = in_part.transpose(1, 3, 0, 2, 4).reshape(sections, tok_dev, row_count // split)
    reduced = lax.psum_scatter(in_part, "section", scatter_dimension=0, tiled=True)
    routes = [
        (s * ranks + k, (split * k + s % split) * ranks + s // split)
        for s in range(sections)
        for k in range(ranks)
    ]
    passed_back = lax.ppermute(reduced, ("section", "dp"), routes)[0]

    grads = jnp.stack(
        [
            lax.dot_general(act_full, back_up, over_tokens, preferred_element_type=F32).astype(BF16),
            lax.dot_general(cot_full, hidden, over_tokens, preferred_element_type=F32).astype(BF16),
        ]
    )
    outgoing = pick_rows(source, grads, block_rows, True)
    arrivals = lax.all_to_all(outgoing, "section", split_axis=0, concat_axis=0, tiled=True)
    updated = adam_slots(
        items,
        count.reshape(1),
        fixes,
        arrivals,
        (master[0, 0], moment_one[0, 0], moment_two[0, 0]),
        0,
    )
    returned = lax.all_to_all(updated, "section", split_axis=0, concat_axis=0, tiled=True)
    new_rows = place_rows(place, [returned], row_blocks)
    return (passed_back, new_rows)


def solution(mesh):
    in_specs = (
        P("dp", None),
        P("dp", None),
        P("dp", "section"),
        P(None, "dp", "section"),
        P("dp", "section", None),
        P("section", "dp", None, None, None),
        P("section", "dp", None, None, None),
        P("section", "dp", None, None, None),
        P(),
    )
    out_specs = (P("dp", "section"), P(None, "dp", "section"))
    return jax.shard_map(
        per_device, mesh=mesh, in_specs=in_specs, out_specs=out_specs, check_vma=False
    )
```

time: 911 us -> 720 us (0.79)
  waiting for transfers between devices: 674 us -> 377 us
  blocking collectives: 7.94 us -> 144 us
  other arithmetic: 83.7 us -> 8.26 us
  Pallas kernels: 0 us -> 66.6 us
  local copies, waits for them, and re-layouts: 70.7 us -> 35 us
  starting transfers between devices: 13.7 us -> 30.3 us
    reduce_scatter x2 -> x3, waiting for transfers between devices: 263 us -> 82.2 us  [the longest x2 82.2 us: project(): lax.psum_scatter(part, 'dp', scatter_dimension=0, tiled=True).astype(F32)]
    all_gather x1 -> x4, waiting for transfers between devices: 291 us -> 160 us  [the longest x2 88.6 us: all_tokens(): out = lax.all_gather(local, 'dp', axis=0, tiled=True)]
    unnamed x1, blocking collectives: 7.94 us -> 84.3 us
    pallas_call x0 -> x3, Pallas kernels: none -> 66.6 us  [the longest x1 30.4 us: pick_rows(): pl.pallas_call(move_kernel, out_shape=jax.ShapeDtypeStruct((count, rows,...]
    all_to_all x0 -> x2, blocking collectives: none -> 60 us  [spread(): swapped = lax.all_to_all(own, 'dp', split_axis=1, concat_axis=0, tiled=True)]
    gather x5 -> x0, local copies, waits for them, and re-layouts: 52.7 us -> none  [the longest x3 38.9 us: per_device(): jnp.take(state, slot_index, axis=0).reshape(arrivals.shape)]
    convert_element_type x3 -> x1, other arithmetic: 38.7 us -> 2.61 us  [per_device(): hidden = all_tokens((gate_silu * lifted).astype(BF16))]
    select_n x13 -> x1, other arithmetic: 34.6 us -> 0.07 us  [per_device(): jnp.where(spot[None, :] < mine[:, None], before[:, None] + spot[None, :],...]
  transfers between devices with their start and end apart: 6 -> 10, of which waited for: 4 -> 7; matrix products, arithmetic and copies ran while one was open for 17% -> 8% of each run, Pallas kernels for 0% -> 2%
where the time goes in v1:
time: 720 us; the launch traced here: 717 us
  waiting for transfers between devices  377 us (52%)
  blocking collectives  144 us (20%)
  Pallas kernels  66.6 us (9%)
  matrix products  38.7 us (5%)
  local copies, waits for them, and re-layouts  35 us (5%)
  starting transfers between devices  30.3 us (4%)
  between operations  16.4 us (2%)
  other arithmetic  8.26 us (1%)
    all_to_all x1, waiting for transfers between devices, per_device(): lax.all_to_all(updated, 'section', split_axis=0, concat_axis=0, tiled=True)  134 us
    all_gather x2, waiting for transfers between devices, all_tokens(): out = lax.all_gather(local, 'dp', axis=0, tiled=True)  88.6 us
    unnamed x1, blocking collectives  84.3 us
    reduce_scatter x2, waiting for transfers between devices, project(): lax.psum_scatter(part, 'dp', scatter_dimension=0, tiled=True).astype(F32)  82.2 us
    all_gather x2, waiting for transfers between devices, spread(): return lax.all_gather(swapped, 'section', axis=0, tiled=True)  71.7 us
    all_to_all x2, blocking collectives, spread(): swapped = lax.all_to_all(own, 'dp', split_axis=1, concat_axis=0, tiled=True)  60 us
    pallas_call x1, Pallas kernels, pick_rows(): pl.pallas_call(move_kernel, out_shape=jax.ShapeDtypeStruct((count, rows,...  30.4 us
    all_to_all x1, starting transfers between devices, per_device(): lax.all_to_all(updated, 'section', split_axis=0, concat_axis=0, tiled=True)  23 us
  transfers between devices with their start and end apart: 10, of which 7 were waited for; matrix products, arithmetic and copies ran while one was open for 8% of the time, Pallas kernels for 2%

profile of v1, /device:TPU:0, one launch (start us, length us, event | category | flops | bytes accessed | tf_op | source)
XLA Modules:
  0.0 716.6 jit_solution(17785833008739846380)
XLA Ops:
  7.2 1.7 constant_dynamic-slice_fusion
  9.0 31.9 %all_to_all.48 = bf16[64,4,2048]{2,0,1:T(8,128)(2,1)} all-to-all(bf16[64,4,2048]{2,0,1:T(8,128)(2,1)S(1)} %bitcast.73), channel_id=1, replica_groups=mesh['section'=8,'dp'=4] {'dp'}, dimensions={1} | all-to-all | bytes 2097152 | tf_op jit(solution)/shard_map/all_to_all | solution.py:150
  41.0 0.1 copy.47
  41.1 28.0 %all_to_all.49 = bf16[64,4,2048]{2,0,1:T(8,128)(2,1)} all-to-all(bf16[64,4,2048]{2,0,1:T(8,128)(2,1)S(1)} %bitcast.74), channel_id=1, replica_groups=mesh['section'=8,'dp'=4] {'dp'}, dimensions={1} | all-to-all | bytes 2097152 | tf_op jit(solution)/shard_map/all_to_all | solution.py:150
  69.2 25.4 %all-gather.6.cloned.1.call-done = bf16[2048,2048]{1,0:T(8,128)(2,1)} async-done(((bf16[256,2048]{1,0:T(8,128)(2,1)}), bf16[2048,2048]{1,0:T(8,128)(2,1)}) %all-gather.6.cloned.1.call-update) | async-done | bytes 8388624 | tf_op jit(solution)/shard_map/all_gather | solution.py:151
  94.6 8.5 %convolution_convert_fusion.4 = bf16[2048,512]{1,0:T(8,128)(2,1)S(1)} fusion(bf16[2048,2048]{1,0:T(8,128)(2,1)} %all-gather.6.cloned.1.call-done, bf16[2,2048,512]{2,1,0:T(8,128)(2,1)} %param.12), kind=kOutput, calls=%fused_computation.5 | convolution fusion | flops 4296015872 | bytes 12582912 | tf_op jit(solution)/shard_map/dot_general | solution.py:154
  103.1 1.5 copy.36
  104.7 46.3 %all-gather.10.cloned.1.call-done = bf16[2048,2048]{1,0:T(8,128)(2,1)} async-done(((bf16[256,2048]{1,0:T(8,128)(2,1)}), bf16[2048,2048]{1,0:T(8,128)(2,1)}) %all-gather.10.cloned.1.call-update) | async-done | bytes 8388624 | tf_op jit(solution)/shard_map/all_gather | solution.py:151
  150.9 8.5 %convolution_convert_fusion.2 = bf16[2048,512]{1,0:T(8,128)(2,1)S(1)} fusion(bf16[2048,2048]{1,0:T(8,128)(2,1)} %all-gather.10.cloned.1.call-done, bf16[2,2048,512]{2,1,0:T(8,128)(2,1)} %param.12), kind=kOutput, calls=%fused_computation.3 | convolution fusion | flops 4296015872 | bytes 12582912 | tf_op jit(solution)/shard_map/dot_general | solution.py:154
  159.4 1.5 copy.41
  161.0 36.1 %reduce-scatter.4.cloned.1.call-done = bf16[512,512]{1,0:T(8,128)(2,1)} async-done(((bf16[2048,512]{1,0:T(8,128)(2,1)}), bf16[512,512]{1,0:T(8,128)(2,1)}) %reduce-scatter.4.cloned.1.call-update) | async-done | bytes 524304 | tf_op jit(solution)/shard_map/reduce_scatter | solution.py:157
  197.1 46.1 %reduce-scatter.8.cloned.1.call-done = bf16[512,512]{1,0:T(8,128)(2,1)} async-done(((bf16[2048,512]{1,0:T(8,128)(2,1)}), bf16[512,512]{1,0:T(8,128)(2,1)}) %reduce-scatter.8.cloned.1.call-update) | async-done | bytes 524304 | tf_op jit(solution)/shard_map/reduce_scatter | solution.py:157
  243.2 2.6 multiply_convert_fusion
  245.8 0.2 all-gather.12.cloned.1.call-start
  246.0 0.3 all-gather.12.cloned.1.call-update
  246.4 0.1 copy.39
  246.5 0.1 reshape_squeeze.3
  246.7 0.2 fusion.12
  246.9 0.7 select_reduce_fusion.1.index_ref
  247.6 43.6 %all-gather.8.cloned.1.call-done = bf16[2048,512]{1,0:T(8,128)(2,1)} async-done(((bf16[512,512]{1,0:T(8,128)(2,1)}), bf16[2048,512]{1,0:T(8,128)(2,1)}) %all-gather.8.cloned.1.call-update) | async-done | bytes 2097168 | tf_op jit(solution)/shard_map/all_gather | solution.py:160
  291.2 1.8 copy.37
  293.0 44.9 %all-gather.12.cloned.1.call-done = bf16[2048,512]{1,0:T(8,128)(2,1)} async-done(((bf16[512,512]{1,0:T(8,128)(2,1)}), bf16[2048,512]{1,0:T(8,128)(2,1)}) %all-gather.12.cloned.1.call-update) | async-done | bytes 2097168 | tf_op jit(solution)/shard_map/all_gather | solution.py:160
  337.9 1.9 copy.42
  339.8 8.6 %fusion = bf16[1,2048,512]{2,1,0:T(8,128)(2,1)S(1)} fusion(bf16[2048,2048]{1,0:T(8,128)(2,1)} %all-gather.10.cloned.1.call-done, bf16[2048,512]{1,0:T(8,128)(2,1)S(1)} %bitcast.77), kind=kOutput, calls=%fused_computation.6 | convolution fusion | flops 4296015872 | bytes 12582912 | tf_op jit(solution)/shard_map/dot_general | solution.py:188
  348.5 4.8 fusion.1
  353.3 2.4 pad_maximum_fusion.in_ref
  355.6 30.4 %pick_rows.1 = bf16[64,128,512]{2,1,0:T(8,128)(2,1)} custom-call(s32[64]{0:T(128)} %select_reduce_fusion.1.index_ref, bf16[2,2048,512]{2,1,0:T(8,128)(2,1)} %pad_maximum_fusion.in_ref), custom_call_target="tpu_custom_call" | custom-call | tf_op jit(solution)/shard_map/pick_rows/pallas_call | solution.py:67
  386.0 4.9 all-to-all-start.2
  391.0 8.3 %convolution_convert_fusion = bf16[2048,2048]{1,0:T(8,128)(2,1)} fusion(bf16[2048,512]{1,0:T(8,128)(2,1)S(1)} %bitcast.78, bf16[2,2048,512]{2,1,0:T(8,128)(2,1)} %param.12), kind=kOutput, calls=%fused_computation | convolution fusion | flops 4299161600 | bytes 12582912 | tf_op jit(solution)/shard_map/dot_general | solution.py:173
  399.3 14.5 %reshape.134 = bf16[8,4,64,2,1024]{4,3,2,1,0:T(2,128)(2,1)} reshape(bf16[2048,2048]{1,0:T(8,128)(2,1)} %convolution_convert_fusion) | data formatting | bytes 16777216 | tf_op jit(solution)/shard_map/reshape | solution.py:176
  413.9 9.3 %copy.38 = bf16[4,2,8,64,1024]{4,3,2,1,0:T(8,128)(2,1)} copy(bf16[4,2,8,64,1024]{4,1,3,0,2:T(2,128)(2,1)} %bitcast.63) | data formatting | bytes 16777216 | tf_op jit(solution)/shard_map/transpose | solution.py:177
  423.2 0.6 copy-done.3
  423.8 0.6 dynamic-slice
  425.1 0.2 dynamic-update-slice
  425.3 84.3 %all-reduce = s32[64]{0:T(128)S(1)} all-reduce(s32[64]{0:T(128)S(1)} %dynamic-update-slice), channel_id=2, replica_groups=mesh['section'=8,'dp'=4] {'section'}, use_global_device_ids=true, to_apply=%add | all-reduce | flops 64 | bytes 512
  509.6 0.1 reshape.143
  509.7 0.7 select_reduce_fusion.3
  510.4 0.2 reduce-window.8
  510.6 0.1 add_select_fusion
  510.7 0.1 select_n.30
  512.1 0.7 pad_maximum_fusion.1.fix_ref
  512.8 0.7 select_reduce_fusion.item_ref
  513.5 17.7 %adam.1 = bf16[64,128,512]{2,1,0:T(8,128)(2,1)} custom-call(s32[48]{0:T(128)} %select_reduce_fusion.item_ref, s32[1]{0:T(128)} %bitcast.16.count_ref, f32[2]{0:T(128)} %pad_maximum_fusion.1.fix_ref, bf16[64,128,512]{2,1,0:T(8,128)(2,1)} %all-to-all-done.2.grad_ref, f32[48,128,512]{2,1,0:T(8,128)} %bitcast.64, f32[48,128,512]{2,1,0:T(8,128)} %bitcast.65, ...), custom_call_target="tpu_custom_call" | custom-call | flops 62914560 | bytes 50331648 | tf_op jit(solution)/shard_map/adam/pallas_call | solution.py:42
  531.2 23.0 %all-to-all-start.3 = ((bf16[64,128,512]{2,1,0:T(8,128)(2,1)}), bf16[64,128,512]{2,1,0:T(8,128)(2,1)}, u32[]{:S(2)}, u32[]{:S(2)}) async-start(bf16[64,128,512]{2,1,0:T(8,128)(2,1)} %adam.1), calls=%async_computation.6 | async-start | bytes 16777216 | tf_op jit(solution)/shard_map/all_to_all | solution.py:202
  554.2 1.9 collective-permute-start
  556.1 134.2 %all-to-all-done.3.refs_0_ = bf16[64,128,512]{2,1,0:T(8,128)(2,1)} async-done(((bf16[64,128,512]{2,1,0:T(8,128)(2,1)}), bf16[64,128,512]{2,1,0:T(8,128)(2,1)}, u32[]{:S(2)}, u32[]{:S(2)}) %all-to-all-start.3) | async-done | bytes 8388640 | tf_op jit(solution)/shard_map/all_to_all | solution.py:202
  690.3 18.5 %place_rows.1 = bf16[2,2048,512]{2,1,0:T(8,128)(2,1)} custom-call(s32[32]{0:T(128)} %copy-done.2, bf16[64,128,512]{2,1,0:T(8,128)(2,1)} %all-to-all-done.3.refs_0_), custom_call_target="tpu_custom_call" | custom-call | tf_op jit(solution)/shard_map/place_rows/pallas_call | solution.py:89
  708.8 1.0 copy.52
  (35 shorter events, 0.6 us)
Async XLA Ops:
  7.2 87.5 %all-gather.6.cloned.1.call-start = ((), (), s32[]{:S(2)}) async-start(), calls=%async_computation.7 | async-start | bytes 9437184 | tf_op jit(solution)/shard_map/all_gather | solution.py:151
  41.0 110.0 %all-gather.10.cloned.1.call-start = ((), (), s32[]{:S(2)}) async-start(), calls=%async_computation.11 | async-start | bytes 9437184 | tf_op jit(solution)/shard_map/all_gather | solution.py:151
  69.2 127.9 %reduce-scatter.4.cloned.1.call-start = ((), (), s32[]{:S(2)}) async-start(), calls=%async_computation.8 | async-start | bytes 2621440 | tf_op jit(solution)/shard_map/reduce_scatter | solution.py:157
  104.6 138.6 %reduce-scatter.8.cloned.1.call-start = ((), (), s32[]{:S(2)}) async-start(), calls=%async_computation.12 | async-start | bytes 2621440 | tf_op jit(solution)/shard_map/reduce_scatter | solution.py:157
  159.4 83.8 %copy-start = (bf16[512,512]{1,0:T(8,128)(2,1)S(1)}, bf16[512,512]{1,0:T(8,128)(2,1)}, u32[]{:S(2)}) copy-start(bf16[512,512]{1,0:T(8,128)(2,1)} %param.11) | copy-start | bytes 1572868
  159.4 87.0 %copy-start.1 = (s32[16,1,2]{0,2,1:T(2,128)S(1)}, s32[16,1,2]{0,2,1:T(2,128)}, u32[]{:S(2)}) copy-start(s32[16,1,2]{0,2,1:T(2,128)} %param.13) | copy-start | bytes 388
  160.9 130.3 %all-gather.8.cloned.1.call-start = ((), (), s32[]{:S(2)}) async-start(), calls=%async_computation.9 | async-start | bytes 2621440 | tf_op jit(solution)/shard_map/all_gather | solution.py:160
  245.8 92.1 %all-gather.12.cloned.1.call-start = ((), (), s32[]{:S(2)}) async-start(), calls=%async_computation.13 | async-start | bytes 2621440 | tf_op jit(solution)/shard_map/all_gather | solution.py:160
  246.9 92.9 %copy-start.2 = (s32[32]{0:T(128)}, s32[32]{0:T(128)S(1)}, u32[]{:S(2)}) copy-start(s32[32]{0:T(128)S(1)} %multiply_add_fusion.index_ref) | copy-start | bytes 388
  337.9 10.5 %slice-start = ((s8[8388608]{0:T(1024)(128)(4,1)}), s8[4194304]{0:T(1024)(128)(4,1)S(1)}, s32[]{:S(2)}) async-start(s8[8388608]{0:T(1024)(128)(4,1)} %bitcast.84), calls=%async_computation.14 | async-start | bytes 8388608
  339.8 8.6 %slice-start.1 = ((s8[8388608]{0:T(1024)(128)(4,1)}), s8[4194304]{0:T(1024)(128)(4,1)S(1)}, s32[]{:S(2)}) async-start(s8[8388608]{0:T(1024)(128)(4,1)} %bitcast.84), calls=%async_computation.15 | async-start | bytes 8388608
  386.0 127.5 %all-to-all-start.2 = ((bf16[64,128,512]{2,1,0:T(8,128)(2,1)}), bf16[64,128,512]{2,1,0:T(8,128)(2,1)}, u32[]{:S(2)}, u32[]{:S(2)}) async-start(bf16[64,128,512]{2,1,0:T(8,128)(2,1)} %pick_rows.1), calls=%async_computation.5 | async-start | bytes 16777216 | tf_op jit(solution)/shard_map/all_to_all | solution.py:193
  391.0 163.2 %reduce-scatter.6.cloned.1.call-start = ((), (), s32[]{:S(2)}) async-start(), calls=%async_computation.10 | async-start | bytes 9437184 | tf_op jit(solution)/shard_map/reduce_scatter | solution.py:178
  423.2 0.7 copy-start.3
  531.2 159.1 %all-to-all-start.3 = ((bf16[64,128,512]{2,1,0:T(8,128)(2,1)}), bf16[64,128,512]{2,1,0:T(8,128)(2,1)}, u32[]{:S(2)}, u32[]{:S(2)}) async-start(bf16[64,128,512]{2,1,0:T(8,128)(2,1)} %adam.1), calls=%async_computation.6 | async-start | bytes 16777216 | tf_op jit(solution)/shard_map/all_to_all | solution.py:202
  554.2 1.9 collective-permute-start
Sparse Core Ops, SparseCore 0:
  41.1 53.4 all-gather.5
  96.5 54.3 all-gather.9
  153.2 43.8 reduce-scatter.3
  199.9 43.1 reduce-scatter.7
  245.9 45.2 all-gather.7
  293.2 44.6 all-gather.11
  423.3 102.0 reduce-scatter.5

commit v2 on v1

v2 whole, which is shorter than its diff:
```python
import jax
import jax.numpy as jnp
from jax import lax
from jax.experimental import pallas as pl
from jax.experimental.pallas import tpu as pltpu
from jax.sharding import PartitionSpec as P

learn_rate = 0.03
beta_one = 0.9
beta_two = 0.95
adam_eps = 1e-08
decay_rate = 0.1

BF16 = jnp.bfloat16
F32 = jnp.float32


CHUNKS = 2
MESH = pl.DeviceIdType.MESH


def spread_kernel(shape, cot_ref, act_ref, cot_out, act_out, local_sem, send_sem, recv_sem):
    sections, ranks, tok_dev, cols = shape
    chips = sections // 2
    piece = tok_dev // sections
    s = lax.axis_index("section")
    k = lax.axis_index("dp")
    core = lax.rem(s, 2)
    chip = s // 2
    sibling = (s + 1 - 2 * core, k)
    along = {d: (s, lax.rem(k + d, ranks)) for d in range(1, ranks)}
    across = {j: (2 * lax.rem(chip + j, chips) + core, k) for j in range(1, chips)}

    barrier = pltpu.get_barrier_semaphore()
    greeted = list(along.values()) + list(across.values()) + [sibling]
    for peer in greeted:
        pl.semaphore_signal(barrier, inc=1, device_id=peer, device_id_type=MESH)
    pl.semaphore_wait(barrier, len(greeted))

    pairs = ((cot_ref, cot_out), (act_ref, act_out))
    sems = iter(range(send_sem.shape[0]))

    def send(src, dst, peer):
        at = next(sems)
        copy = pltpu.make_async_remote_copy(
            src_ref=src,
            dst_ref=dst,
            send_sem=send_sem.at[at],
            recv_sem=recv_sem.at[at],
            device_id=peer,
            device_id_type=MESH,
        )
        copy.start()
        return copy

    def rows(out, rank, section):
        start = pl.multiple_of(rank * tok_dev + section * piece, piece)
        return out.at[pl.ds(start, piece), :]

    hops = {}
    for d in range(1, ranks):
        for a, (ref, out) in enumerate(pairs):
            start = pl.multiple_of(along[d][1] * cols, cols)
            from_rows = pl.ds(pl.multiple_of(s * piece, piece), piece)
            hops[a, d] = send(ref.at[from_rows, pl.ds(start, cols)], rows(out, k, s), along[d])
    local = []
    for a, (ref, out) in enumerate(pairs):
        copy = pltpu.make_async_copy(
            ref.at[:, pl.ds(pl.multiple_of(k * cols, cols), cols)],
            out.at[pl.ds(pl.multiple_of(k * tok_dev, tok_dev), tok_dev), :],
            local_sem.at[a],
        )
        copy.start()
        local.append(copy)
    wide, last = {}, []
    for d in range(1, ranks):
        origin = lax.rem(k + ranks - d, ranks)
        for a, (ref, out) in enumerate(pairs):
            hops[a, d].wait_recv()
            block = rows(out, origin, s)
            for j in range(1, chips):
                wide[a, d, j] = send(block, block, across[j])
            last.append(send(block, block, sibling))
    for d in range(1, ranks):
        origin = lax.rem(k + ranks - d, ranks)
        for a, (ref, out) in enumerate(pairs):
            for j in range(1, chips):
                wide[a, d, j].wait_recv()
                block = rows(out, origin, 2 * lax.rem(chip + chips - j, chips) + core)
                last.append(send(block, block, sibling))
    for copy in last:
        copy.wait_recv()
    for copy in list(hops.values()) + list(wide.values()) + last:
        copy.wait_send()
    for copy in local:
        copy.wait()


def spread(cotangent, activations, sections, ranks):
    tok_dev, width = activations.shape
    cols = width // ranks
    copies = 2 * (ranks - 1) * sections
    out = jax.ShapeDtypeStruct((ranks * tok_dev, cols), activations.dtype)
    anywhere = pl.BlockSpec(memory_space=pl.ANY)
    moved = 2 * ranks * tok_dev * cols * 2

    def body(*refs):
        spread_kernel((sections, ranks, tok_dev, cols), *refs)

    return pl.pallas_call(
        body,
        out_shape=(out, out),
        in_specs=[anywhere, anywhere],
        out_specs=(anywhere, anywhere),
        scratch_shapes=[
            pltpu.SemaphoreType.DMA((2,)),
            pltpu.SemaphoreType.DMA((copies,)),
            pltpu.SemaphoreType.DMA((copies,)),
        ],
        compiler_params=pltpu.CompilerParams(collective_id=1, has_side_effects=True),
        cost_estimate=pl.CostEstimate(flops=0, bytes_accessed=8 * moved, transcendentals=0),
        name="spread",
    )(cotangent, activations)


def adam_kernel(source_ref, count_ref, fix_ref, grad_ref, w_ref, a_ref, b_ref, out_ref):
    @pl.when(pl.program_id(0) < count_ref[0])
    def _():
        scale_one = learn_rate / fix_ref[0]
        scale_two = 1.0 / fix_ref[1]

        def one(i, carry):
            grad = grad_ref[i].astype(F32)
            first = beta_one * a_ref[i] + (1.0 - beta_one) * grad
            second = beta_two * b_ref[i] + (1.0 - beta_two) * grad * grad
            update = (first * scale_one) / (jnp.sqrt(second * scale_two) + adam_eps)
            out_ref[i] = (w_ref[i] * (1.0 - learn_rate * decay_rate) - update).astype(BF16)
            return carry

        lax.fori_loop(0, grad_ref.shape[0], one, 0)


def adam_slots(sources, count, fixes, arrivals, states, chunk, per_dest):
    total, rows, cols = arrivals.shape
    capacity = states[0].shape[0]
    groups = capacity // per_dest
    cuts = 2

    def at_slot(g, h, source_ref, count_ref):
        live = g < count_ref[0]
        return (
            jnp.minimum(g, jnp.maximum(count_ref[0] - 1, 0)),
            jnp.where(live, h, cuts - 1),
            chunk,
        )

    def at_item(g, h, source_ref, count_ref):
        return (source_ref[g], jnp.where(g < count_ref[0], h, cuts - 1), 0)

    state_spec = pl.BlockSpec((per_dest, rows // cuts, cols), at_slot)
    item_spec = pl.BlockSpec((per_dest, rows // cuts, cols), at_item)
    return pl.pallas_call(
        adam_kernel,
        out_shape=jax.ShapeDtypeStruct(arrivals.shape, BF16),
        grid_spec=pltpu.PrefetchScalarGridSpec(
            num_scalar_prefetch=2,
            grid=(groups, cuts),
            in_specs=[pl.BlockSpec(memory_space=pltpu.SMEM), item_spec] + [state_spec] * 3,
            out_specs=item_spec,
        ),
        cost_estimate=pl.CostEstimate(
            flops=20 * capacity * rows * cols,
            bytes_accessed=16 * capacity * rows * cols,
            transcendentals=capacity * rows * cols,
        ),
        name="adam",
    )(sources, count, fixes, arrivals, *states)


def pick_rows(place, grads, rows, slots):
    cols = grads[0].shape[1]
    count = place.shape[0]
    anywhere = pl.BlockSpec(memory_space=pl.ANY)

    def body(place_ref, up_ref, down_ref, out_ref, sems):
        copies = []
        for i in range(count):
            ref = (up_ref, down_ref)[i % 2]
            copy = pltpu.make_async_copy(
                ref.at[pl.ds(i // 2 * rows, rows), :], out_ref.at[place_ref[i]], sems.at[i]
            )
            copy.start()
            copies.append(copy)
        for copy in copies:
            copy.wait()

    return pl.pallas_call(
        body,
        out_shape=jax.ShapeDtypeStruct((slots, rows, cols), grads[0].dtype),
        in_specs=[pl.BlockSpec(memory_space=pltpu.SMEM), anywhere, anywhere],
        out_specs=anywhere,
        scratch_shapes=[pltpu.SemaphoreType.DMA((count,))],
        cost_estimate=pl.CostEstimate(
            flops=0, bytes_accessed=4 * count * rows * cols, transcendentals=0
        ),
        name="pick_rows",
    )(place, *grads)


def place_rows(place, parts, row_blocks):
    rows, cols = parts[0].shape[1:]
    width = cols * len(parts)
    count = row_blocks * 2
    anywhere = pl.BlockSpec(memory_space=pl.ANY)

    def body(place_ref, *refs):
        out_ref, sems = refs[-2:]
        copies = []
        for at, ref in enumerate(refs[:-2]):
            for i in range(count):
                copy = pltpu.make_async_copy(
                    ref.at[place_ref[i]],
                    out_ref.at[i % 2, pl.ds(i // 2 * rows, rows), pl.ds(at * cols, cols)],
                    sems.at[at * count + i],
                )
                copy.start()
                copies.append(copy)
        for copy in copies:
            copy.wait()

    return pl.pallas_call(
        body,
        out_shape=jax.ShapeDtypeStruct((2, row_blocks * rows, width), parts[0].dtype),
        in_specs=[pl.BlockSpec(memory_space=pltpu.SMEM)] + [anywhere] * len(parts),
        out_specs=anywhere,
        scratch_shapes=[pltpu.SemaphoreType.DMA((count * len(parts),))],
        cost_estimate=pl.CostEstimate(
            flops=0, bytes_accessed=4 * count * rows * width, transcendentals=0
        ),
        name="place_rows",
    )(place, *parts)


def per_device(
    activations, cotangent, gate_pre, weights, holder_map, master, moment_one, moment_two, adam_step
):
    sections = lax.axis_size("section")
    ranks = lax.axis_size("dp")
    here = lax.axis_index("section")
    tok_dev, width = activations.shape
    row_count, hidden_units = weights.shape[1:]
    block_rows = master.shape[3]
    capacity = master.shape[2]
    row_blocks = row_count // block_rows
    per_dest = 4 * row_blocks // sections
    over_tokens = (((0,), (0,)), ((), ()))
    span = hidden_units // CHUNKS if hidden_units % (128 * CHUNKS) == 0 else hidden_units
    chunks = hidden_units // span

    owners = holder_map[:, 0, :].reshape(-1)
    section_ids = jnp.arange(sections, dtype=jnp.int32)
    choose = (owners[:, None] == section_ids[None, :]).astype(jnp.int32)
    totals = jnp.sum(choose, axis=0)
    every_total = lax.all_gather(totals, "section")
    every_total, activations, cotangent = lax.optimization_barrier(
        (every_total, activations, cotangent)
    )
    order_in = jnp.sum((jnp.cumsum(choose, axis=0) - choose) * choose, axis=1)
    place = owners * per_dest + order_in
    mine = jnp.sum(jnp.where(section_ids[None, :] == here, every_total, 0), axis=1)
    live = (mine > 0).astype(jnp.int32)
    rank_of = jnp.cumsum(live) - live
    count = jnp.sum(live)
    groups = jnp.minimum(
        jnp.arange(capacity // per_dest, dtype=jnp.int32), jnp.maximum(count - 1, 0)
    )
    sources = jnp.sum(
        jnp.where(
            (rank_of[None, :] == groups[:, None]) & (live[None, :] > 0), section_ids[None, :], 0
        ),
        axis=1,
    )
    step_float = adam_step[0].astype(F32)
    fixes = jnp.stack(
        [
            1.0 - jnp.power(jnp.float32(beta_one), step_float),
            1.0 - jnp.power(jnp.float32(beta_two), step_float),
        ]
    )
    states = (master[0, 0], moment_one[0, 0], moment_two[0, 0])
    gate_silu = jax.nn.silu(gate_pre.astype(F32))

    cot_full, act_full = spread(cotangent, activations, sections, ranks)

    gathered = []
    for j in range(chunks):
        at = slice(j * span, (j + 1) * span)
        part = jnp.concatenate(
            [
                jnp.dot(cot_full, weights[1][:, at], preferred_element_type=F32).astype(BF16),
                jnp.dot(act_full, weights[0][:, at], preferred_element_type=F32).astype(BF16),
            ],
            axis=1,
        )
        both = lax.psum_scatter(part, "dp", scatter_dimension=0, tiled=True).astype(F32)
        gate = gate_silu[:, at]
        local = (both * jnp.concatenate([gate, gate], axis=1)).astype(BF16)
        gathered.append(lax.all_gather(local, "dp", axis=0, tiled=True))

    returned = []
    for j in range(chunks):
        grads = (
            lax.dot_general(
                act_full, gathered[j][:, :span], over_tokens, preferred_element_type=F32
            ).astype(BF16),
            lax.dot_general(
                cot_full, gathered[j][:, span:], over_tokens, preferred_element_type=F32
            ).astype(BF16),
        )
        outgoing = pick_rows(place, grads, block_rows, sections * per_dest)
        arrivals = lax.all_to_all(outgoing, "section", split_axis=0, concat_axis=0, tiled=True)
        updated = adam_slots(sources, count.reshape(1), fixes, arrivals, states, j, per_dest)
        returned.append(
            lax.all_to_all(updated, "section", split_axis=0, concat_axis=0, tiled=True)
        )

    split = sections // ranks
    back_up = jnp.concatenate([each[:, :span] for each in gathered], axis=1)
    back_up = back_up.reshape(ranks, tok_dev, hidden_units)
    up_rows = weights[0].reshape(split, row_count // split, hidden_units)
    in_part = jnp.stack(
        [
            lax.dot_general(
                back_up[i // split],
                up_rows[i % split],
                (((1,), (1,)), ((), ())),
                preferred_element_type=F32,
            ).astype(BF16)
            for i in range(sections)
        ]
    )
    reduced = lax.psum_scatter(in_part, "section", scatter_dimension=0, tiled=True)
    routes = [
        (s * ranks + k, (split * k + s % split) * ranks + s // split)
        for s in range(sections)
        for k in range(ranks)
    ]
    passed_back = lax.ppermute(reduced, ("section", "dp"), routes)[0]

    new_rows = place_rows(place, returned, row_blocks)
    return (passed_back, new_rows)


def solution(mesh):
    in_specs = (
        P("dp", None),
        P("dp", None),
        P("dp", "section"),
        P(None, "dp", "section"),
        P("dp", "section", None),
        P("section", "dp", None, None, None),
        P("section", "dp", None, None, None),
        P("section", "dp", None, None, None),
        P(),
    )
    out_specs = (P("dp", "section"), P(None, "dp", "section"))
    return jax.shard_map(
        per_device, mesh=mesh, in_specs=in_specs, out_specs=out_specs, check_vma=False
    )
```

time: 720 us -> 828 us (1.15)
  Pallas kernels: 66.6 us -> 409 us
  blocking collectives: 144 us -> 9.46 us
  waiting for transfers between devices: 377 us -> 285 us
  matrix products: 38.7 us -> 65.5 us
  local copies, waits for them, and re-layouts: 35 us -> 10.6 us
  starting transfers between devices: 30.3 us -> 20.5 us
    pallas_call x1 -> x3, Pallas kernels: 30.4 us -> 264 us  [the longest x1 133 us: spread(): pl.pallas_call(body, out_shape=(out, out), in_specs=[anywhere, anywhere],...]
    all_gather x4 -> x2, waiting for transfers between devices: 160 us -> 45 us  [per_device(): gathered.append(lax.all_gather(local, 'dp', axis=0, tiled=True))]
    pallas_call x1, Pallas kernels: 18.5 us -> 129 us  [place_rows(): pl.pallas_call(body, out_shape=jax.ShapeDtypeStruct((2, row_blocks * rows...]
    unnamed x1, blocking collectives: 84.3 us -> 9.46 us
    all_to_all x2 -> x0, blocking collectives: 60 us -> none  [spread(): swapped = lax.all_to_all(own, 'dp', split_axis=1, concat_axis=0, tiled=True)]
    all_to_all x1 -> x2, waiting for transfers between devices: 0.01 us -> 37.3 us  [per_device(): lax.all_to_all(outgoing, 'section', split_axis=0, concat_axis=0, tiled=True)]
    dot_general x5 -> x16, matrix products: 38.7 us -> 65.5 us  [the longest x2 15.5 us: per_device(): lax.dot_general(cot_full, gathered[j][:, span:], over_tokens, preferred_e...]
    transpose x5 -> x0, local copies, waits for them, and re-layouts: 15.9 us -> none  [the longest x1 9.31 us: per_device(): in_part.transpose(1, 3, 0, 2, 4)]
  transfers between devices with their start and end apart: 10 -> 10, of which waited for: 7 -> 6; matrix products, arithmetic and copies ran while one was open for 8% -> 8% of each run, Pallas kernels for 2% -> 33%
where the time goes in v2:
time: 828 us; the launch traced here: 827 us
  Pallas kernels  409 us (49%)
  waiting for transfers between devices  285 us (34%)
  matrix products  65.5 us (8%)
  starting transfers between devices  20.5 us (2%)
  between operations  16.1 us (2%)
  local copies, waits for them, and re-layouts  10.6 us (1%)
  other arithmetic  10.3 us (1%)
  blocking collectives  9.46 us (1%)
    pallas_call x1, Pallas kernels, spread(): pl.pallas_call(body, out_shape=(out, out), in_specs=[anywhere, anywhere],...  133 us
    pallas_call x2, Pallas kernels, pick_rows(): pl.pallas_call(body, out_shape=jax.ShapeDtypeStruct((slots, rows, cols),...  131 us
    all_to_all x2, waiting for transfers between devices, per_device(): lax.all_to_all(updated, 'section', split_axis=0, concat_axis=0, tiled=True)  130 us
    pallas_call x1, Pallas kernels, place_rows(): pl.pallas_call(body, out_shape=jax.ShapeDtypeStruct((2, row_blocks * rows...  129 us
    reduce_scatter x2, waiting for transfers between devices, per_device(): lax.psum_scatter(part, 'dp', scatter_dimension=0, tiled=True).astype(F32)  72.2 us
    all_gather x2, waiting for transfers between devices, per_device(): gathered.append(lax.all_gather(local, 'dp', axis=0, tiled=True))  45 us
    all_to_all x2, waiting for transfers between devices, per_device(): lax.all_to_all(outgoing, 'section', split_axis=0, concat_axis=0, tiled=True)  37.3 us
  transfers between devices with their start and end apart: 10, of which 6 were waited for; matrix products, arithmetic and copies ran while one was open for 8% of the time, Pallas kernels for 33%

profile of v2, /device:TPU:0, one launch (start us, length us, event | category | flops | bytes accessed | tf_op | source)
XLA Modules:
  0.0 826.6 jit_solution(8411181487699102869)
XLA Ops:
  7.2 0.8 copy.15
  8.4 1.2 dynamic-slice
  10.5 9.5 %all-reduce = s32[64]{0:T(128)S(1)} all-reduce(s32[64]{0:T(128)S(1)} %dynamic-update-slice), channel_id=2, replica_groups=mesh['section'=8,'dp'=4] {'section'}, use_global_device_ids=true, to_apply=%add | all-reduce | flops 64 | bytes 512
  20.1 3.8 slice_bitcast_fusion.1
  23.9 132.6 %spread.1 = (bf16[2048,2048]{1,0:T(8,128)(2,1)}, bf16[2048,2048]{1,0:T(8,128)(2,1)}) custom-call(bf16[512,8192]{1,0:T(8,128)(2,1)} %refs_0_, bf16[512,8192]{1,0:T(8,128)(2,1)} %refs_1_), custom_call_target="tpu_custom_call" | custom-call | bytes 134217728 | tf_op jit(solution)/shard_map/spread/pallas_call | solution.py:110
  156.5 6.1 convolution_convert_fusion.7
  162.7 2.4 convolution_convert_fusion.6
  165.1 1.5 pad_maximum_fusion
  166.6 6.0 convolution_convert_fusion.5
  172.6 5.8 convolution_convert_fusion.4
  178.4 1.5 pad_maximum_fusion.1
  180.7 28.0 %reduce-scatter.4.cloned.1.call-done = bf16[512,512]{0,1:T(8,128)(2,1)} async-done(((bf16[2048,512]{0,1:T(8,128)(2,1)}), bf16[512,512]{0,1:T(8,128)(2,1)}) %reduce-scatter.4.cloned.1.call-update) | async-done | bytes 524304 | tf_op jit(solution)/shard_map/reduce_scatter | solution.py:305
  208.7 2.0 fusion.25
  210.8 44.1 %reduce-scatter.6.cloned.1.call-done = bf16[512,512]{0,1:T(8,128)(2,1)} async-done(((bf16[2048,512]{0,1:T(8,128)(2,1)}), bf16[512,512]{0,1:T(8,128)(2,1)}) %reduce-scatter.6.cloned.1.call-update) | async-done | bytes 524304 | tf_op jit(solution)/shard_map/reduce_scatter | solution.py:305
  254.9 1.9 fusion.26
  256.9 0.5 multiply_add_fusion.place_ref
  257.4 45.0 %all-gather.4.cloned.1.call-done = bf16[2048,512]{0,1:T(8,128)(2,1)} async-done(((bf16[512,512]{0,1:T(8,128)(2,1)}), bf16[2048,512]{0,1:T(8,128)(2,1)}) %all-gather.4.cloned.1.call-update) | async-done | bytes 2097168 | tf_op jit(solution)/shard_map/all_gather | solution.py:308
  302.3 7.3 convolution_convert_fusion.3.up_ref
  309.6 7.1 convolution_convert_fusion.2.down_ref
  316.8 65.6 %pick_rows.2 = bf16[64,128,256]{2,1,0:T(8,128)(2,1)} custom-call(s32[32]{0:T(128)} %multiply_add_fusion.place_ref, bf16[2048,256]{1,0:T(8,128)(2,1)} %convolution_convert_fusion.3.up_ref, bf16[2048,256]{1,0:T(8,128)(2,1)} %convolution_convert_fusion.2.down_ref), custom_call_target="tpu_custom_call" | custom-call | bytes 4194304 | tf_op jit(solution)/shard_map/pick_rows/pallas_call | solution.py:197
  382.3 4.6 all-to-all-start
  387.2 1.5 slice.102
  388.6 3.1 fusion.1
  391.7 1.8 fusion.3
  393.5 1.8 fusion.5
  395.3 1.7 fusion.7
  397.0 1.7 fusion.9
  398.8 1.8 fusion.11
  400.6 1.8 fusion.13
  402.3 1.7 fusion.15
  404.1 1.6 copy-done.1
  405.7 7.0 convolution_convert_fusion.1.up_ref
  412.7 8.4 %convolution_convert_fusion.down_ref = bf16[2048,256]{1,0:T(8,128)(2,1)} fusion(bf16[2048,2048]{1,0:T(8,128)(2,1)} %get-tuple-element.9, bf16[2048,512]{0,1:T(8,128)(2,1)S(1)} %copy-done.1), kind=kOutput, calls=%fused_computation.6 | convolution fusion | flops 2148007936 | bytes 10485760 | tf_op jit(solution)/shard_map/dot_general | solution.py:316
  421.1 65.6 %pick_rows.3 = bf16[64,128,256]{2,1,0:T(8,128)(2,1)} custom-call(s32[32]{0:T(128)} %multiply_add_fusion.place_ref, bf16[2048,256]{1,0:T(8,128)(2,1)} %convolution_convert_fusion.1.up_ref, bf16[2048,256]{1,0:T(8,128)(2,1)} %convolution_convert_fusion.down_ref), custom_call_target="tpu_custom_call" | custom-call | bytes 4194304 | tf_op jit(solution)/shard_map/pick_rows/pallas_call | solution.py:197
  486.7 4.6 all-to-all-start.2
  492.3 0.6 fusion.48
  493.6 0.6 pad_maximum_fusion.3.fix_ref
  494.2 0.8 select_reduce_fusion.1.source_ref
  495.0 8.1 adam.2
  503.1 37.3 %all-to-all-done.2.grad_ref = bf16[64,128,256]{2,1,0:T(8,128)(2,1)} async-done(((bf16[64,128,256]{2,1,0:T(8,128)(2,1)}), bf16[64,128,256]{2,1,0:T(8,128)(2,1)}, u32[]{:S(2)}, u32[]{:S(2)}) %all-to-all-start.2) | async-done | bytes 4194336 | tf_op jit(solution)/shard_map/all_to_all | solution.py:321
  540.4 4.5 all-to-all-start.1
  545.0 8.2 adam.3
  553.1 41.0 %all-to-all-done.1.refs_0_ = bf16[64,128,256]{2,1,0:T(8,128)(2,1)} async-done(((bf16[64,128,256]{2,1,0:T(8,128)(2,1)}), bf16[64,128,256]{2,1,0:T(8,128)(2,1)}, u32[]{:S(2)}, u32[]{:S(2)}) %all-to-all-start.1) | async-done | bytes 4194336 | tf_op jit(solution)/shard_map/all_to_all | solution.py:324
  594.1 4.5 all-to-all-start.3
  598.7 1.9 collective-permute-start
  600.5 89.1 %all-to-all-done.3.refs_1_ = bf16[64,128,256]{2,1,0:T(8,128)(2,1)} async-done(((bf16[64,128,256]{2,1,0:T(8,128)(2,1)}), bf16[64,128,256]{2,1,0:T(8,128)(2,1)}, u32[]{:S(2)}, u32[]{:S(2)}) %all-to-all-start.3) | async-done | bytes 4194336 | tf_op jit(solution)/shard_map/all_to_all | solution.py:324
  689.7 129.4 %place_rows.1 = bf16[2,2048,512]{2,1,0:T(8,128)(2,1)} custom-call(s32[32]{0:T(128)} %multiply_add_fusion.place_ref, bf16[64,128,256]{2,1,0:T(8,128)(2,1)} %all-to-all-done.1.refs_0_, bf16[64,128,256]{2,1,0:T(8,128)(2,1)} %all-to-all-done.3.refs_1_), custom_call_target="tpu_custom_call" | custom-call | bytes 8388608 | tf_op jit(solution)/shard_map/place_rows/pallas_call | solution.py:231
  819.1 1.0 copy.27
  (40 shorter events, 2.3 us)
Async XLA Ops:
  7.2 201.6 %reduce-scatter.4.cloned.1.call-start = ((), (), s32[]{:S(2)}) async-start(), calls=%async_computation.7 | async-start | bytes 2621440 | tf_op jit(solution)/shard_map/reduce_scatter | solution.py:305
  156.5 6.2 copy-start.4
  166.6 88.3 %reduce-scatter.6.cloned.1.call-start = ((), (), s32[]{:S(2)}) async-start(), calls=%async_computation.9 | async-start | bytes 2621440 | tf_op jit(solution)/shard_map/reduce_scatter | solution.py:305
  178.4 1.7 copy-start.3
  179.9 122.5 %all-gather.4.cloned.1.call-start = ((), (), s32[]{:S(2)}) async-start(), calls=%async_computation.8 | async-start | bytes 2621440 | tf_op jit(solution)/shard_map/all_gather | solution.py:308
  210.7 176.4 %all-gather.6.cloned.1.call-start = ((), (), s32[]{:S(2)}) async-start(), calls=%async_computation.10 | async-start | bytes 2621440 | tf_op jit(solution)/shard_map/all_gather | solution.py:308
  302.3 7.3 copy-start.2
  382.3 104.4 %all-to-all-start = ((bf16[64,128,256]{2,1,0:T(8,128)(2,1)}), bf16[64,128,256]{2,1,0:T(8,128)(2,1)}, u32[]{:S(2)}, u32[]{:S(2)}) async-start(bf16[64,128,256]{2,1,0:T(8,128)(2,1)} %pick_rows.2), calls=%async_computation.3 | async-start | bytes 8388608 | tf_op jit(solution)/shard_map/all_to_all | solution.py:321
  387.0 211.7 %reduce-scatter.8.cloned.1.call-start = ((), (), s32[]{:S(2)}) async-start(), calls=%async_computation.11 | async-start | bytes 9437184 | tf_op jit(solution)/shard_map/reduce_scatter | solution.py:342
  387.2 4.6 copy-start
  404.1 1.6 copy-start.1
  486.7 53.7 %all-to-all-start.2 = ((bf16[64,128,256]{2,1,0:T(8,128)(2,1)}), bf16[64,128,256]{2,1,0:T(8,128)(2,1)}, u32[]{:S(2)}, u32[]{:S(2)}) async-start(bf16[64,128,256]{2,1,0:T(8,128)(2,1)} %pick_rows.3), calls=%async_computation.5 | async-start | bytes 8388608 | tf_op jit(solution)/shard_map/all_to_all | solution.py:321
  540.4 53.7 %all-to-all-start.1 = ((bf16[64,128,256]{2,1,0:T(8,128)(2,1)}), bf16[64,128,256]{2,1,0:T(8,128)(2,1)}, u32[]{:S(2)}, u32[]{:S(2)}) async-start(bf16[64,128,256]{2,1,0:T(8,128)(2,1)} %adam.2), calls=%async_computation.4 | async-start | bytes 8388608 | tf_op jit(solution)/shard_map/all_to_all | solution.py:324
  594.1 95.6 %all-to-all-start.3 = ((bf16[64,128,256]{2,1,0:T(8,128)(2,1)}), bf16[64,128,256]{2,1,0:T(8,128)(2,1)}, u32[]{:S(2)}, u32[]{:S(2)}) async-start(bf16[64,128,256]{2,1,0:T(8,128)(2,1)} %adam.3), calls=%async_computation.6 | async-start | bytes 8388608 | tf_op jit(solution)/shard_map/all_to_all | solution.py:324
  598.7 220.4 %collective-permute-start = (bf16[1,512,1024]{2,1,0:T(8,128)(2,1)}, bf16[1,512,1024]{2,1,0:T(8,128)(2,1)S(1)}, u32[]{:S(2)}, u32[]{:S(2)}) collective-permute-start(bf16[1,512,1024]{2,1,0:T(8,128)(2,1)} %reduce-scatter.8.cloned.1.call-done), channel_id=1, source_target_pairs={{0,0},{1,8},{2,16},{3,24},{4,4},{5,12},{6,20},{7,28},{8,1},{9,9},{... | collective-permute-start | bytes 3145736 | tf_op jit(solution)/shard_map/ppermute | solution.py:348
Sparse Core Ops, SparseCore 0:
  166.7 41.9 reduce-scatter.3
  211.7 43.1 reduce-scatter.5
  257.0 45.2 all-gather.3
  303.8 44.6 all-gather.5
  404.2 72.8 reduce-scatter.7

commit v3 on v2

--- a/solution.py
+++ b/solution.py
@@ -19,7 +19,7 @@
 MESH = pl.DeviceIdType.MESH
 
 
-def spread_kernel(shape, cot_ref, act_ref, cot_out, act_out, local_sem, send_sem, recv_sem):
+def spread_kernel(shape, cot_ref, act_ref, cot_out, act_out, held, local_sem, send_sem, recv_sem):
     sections, ranks, tok_dev, cols = shape
     chips = sections // 2
     piece = tok_dev // sections
@@ -63,15 +63,17 @@
             start = pl.multiple_of(along[d][1] * cols, cols)
             from_rows = pl.ds(pl.multiple_of(s * piece, piece), piece)
             hops[a, d] = send(ref.at[from_rows, pl.ds(start, cols)], rows(out, k, s), along[d])
+    own_cols = pl.ds(pl.multiple_of(k * cols, cols), cols)
+    own_rows = pl.ds(pl.multiple_of(k * tok_dev, tok_dev), tok_dev)
     local = []
     for a, (ref, out) in enumerate(pairs):
-        copy = pltpu.make_async_copy(
-            ref.at[:, pl.ds(pl.multiple_of(k * cols, cols), cols)],
-            out.at[pl.ds(pl.multiple_of(k * tok_dev, tok_dev), tok_dev), :],
-            local_sem.at[a],
-        )
+        copy = pltpu.make_async_copy(ref.at[:, own_cols], held.at[a], local_sem.at[a])
         copy.start()
         local.append(copy)
+    for a, (ref, out) in enumerate(pairs):
+        local[a].wait()
+        local[a] = pltpu.make_async_copy(held.at[a], out.at[own_rows, :], local_sem.at[2 + a])
+        local[a].start()
     wide, last = {}, []
     for d in range(1, ranks):
         origin = lax.rem(k + ranks - d, ranks)
@@ -113,7 +115,8 @@
         in_specs=[anywhere, anywhere],
         out_specs=(anywhere, anywhere),
         scratch_shapes=[
-            pltpu.SemaphoreType.DMA((2,)),
+            pltpu.VMEM((2, tok_dev, cols), activations.dtype),
+            pltpu.SemaphoreType.DMA((4,)),
             pltpu.SemaphoreType.DMA((copies,)),
             pltpu.SemaphoreType.DMA((copies,)),
         ],
@@ -183,21 +186,34 @@
     anywhere = pl.BlockSpec(memory_space=pl.ANY)
 
     def body(place_ref, up_ref, down_ref, out_ref, sems):
-        copies = []
-        for i in range(count):
-            ref = (up_ref, down_ref)[i % 2]
-            copy = pltpu.make_async_copy(
-                ref.at[pl.ds(i // 2 * rows, rows), :], out_ref.at[place_ref[i]], sems.at[i]
+        def copy_of(r, m):
+            ref = (up_ref, down_ref)[m]
+            start = pl.multiple_of(r * rows, rows)
+            return pltpu.make_async_copy(
+                ref.at[pl.ds(start, rows), :], out_ref.at[place_ref[2 * r + m]], sems.at[2 * r + m]
             )
-            copy.start()
-            copies.append(copy)
-        for copy in copies:
-            copy.wait()
+
+        def begin(r, carry):
+            copy_of(r, 0).start()
+            copy_of(r, 1).start()
+            return carry
+
+        def finish(r, carry):
+            copy_of(r, 0).wait()
+            copy_of(r, 1).wait()
+            return carry
+
+        lax.fori_loop(0, count // 2, begin, 0)
+        lax.fori_loop(0, count // 2, finish, 0)
 
     return pl.pallas_call(
         body,
         out_shape=jax.ShapeDtypeStruct((slots, rows, cols), grads[0].dtype),
-        in_specs=[pl.BlockSpec(memory_space=pltpu.SMEM), anywhere, anywhere],
+        in_specs=[
+            pl.BlockSpec(memory_space=pltpu.SMEM),
+            pl.BlockSpec(memory_space=pltpu.VMEM),
+            pl.BlockSpec(memory_space=pltpu.VMEM),
+        ],
         out_specs=anywhere,
         scratch_shapes=[pltpu.SemaphoreType.DMA((count,))],
         cost_estimate=pl.CostEstimate(
@@ -215,24 +231,37 @@
 
     def body(place_ref, *refs):
         out_ref, sems = refs[-2:]
-        copies = []
-        for at, ref in enumerate(refs[:-2]):
-            for i in range(count):
-                copy = pltpu.make_async_copy(
-                    ref.at[place_ref[i]],
-                    out_ref.at[i % 2, pl.ds(i // 2 * rows, rows), pl.ds(at * cols, cols)],
-                    sems.at[at * count + i],
+
+        def copies_of(r):
+            start = pl.multiple_of(r * rows, rows)
+            return [
+                pltpu.make_async_copy(
+                    ref.at[place_ref[2 * r + m]],
+                    out_ref.at[m, pl.ds(start, rows), pl.ds(at * cols, cols)],
+                    sems.at[at * count + 2 * r + m],
                 )
+                for at, ref in enumerate(refs[:-2])
+                for m in range(2)
+            ]
+
+        def begin(r, carry):
+            for copy in copies_of(r):
                 copy.start()
-                copies.append(copy)
-        for copy in copies:
-            copy.wait()
+            return carry
+
+        def finish(r, carry):
+            for copy in copies_of(r):
+                copy.wait()
+            return carry
+
+        lax.fori_loop(0, row_blocks, begin, 0)
+        lax.fori_loop(0, row_blocks, finish, 0)
 
     return pl.pallas_call(
         body,
         out_shape=jax.ShapeDtypeStruct((2, row_blocks * rows, width), parts[0].dtype),
         in_specs=[pl.BlockSpec(memory_space=pltpu.SMEM)] + [anywhere] * len(parts),
-        out_specs=anywhere,
+        out_specs=pl.BlockSpec(memory_space=pltpu.VMEM),
         scratch_shapes=[pltpu.SemaphoreType.DMA((count * len(parts),))],
         cost_estimate=pl.CostEstimate(
             flops=0, bytes_accessed=4 * count * rows * width, transcendentals=0
@@ -292,23 +321,30 @@
 
     cot_full, act_full = spread(cotangent, activations, sections, ranks)
 
-    gathered = []
+    parts = []
     for j in range(chunks):
         at = slice(j * span, (j + 1) * span)
-        part = jnp.concatenate(
-            [
-                jnp.dot(cot_full, weights[1][:, at], preferred_element_type=F32).astype(BF16),
-                jnp.dot(act_full, weights[0][:, at], preferred_element_type=F32).astype(BF16),
-            ],
-            axis=1,
+        parts.append(
+            jnp.concatenate(
+                [
+                    jnp.dot(cot_full, weights[1][:, at], preferred_element_type=F32).astype(BF16),
+                    jnp.dot(act_full, weights[0][:, at], preferred_element_type=F32).astype(BF16),
+                ],
+                axis=1,
+            )
         )
+
+    def sum_and_gather(part, gate):
         both = lax.psum_scatter(part, "dp", scatter_dimension=0, tiled=True).astype(F32)
-        gate = gate_silu[:, at]
         local = (both * jnp.concatenate([gate, gate], axis=1)).astype(BF16)
-        gathered.append(lax.all_gather(local, "dp", axis=0, tiled=True))
-
-    returned = []
+        return lax.all_gather(local, "dp", axis=0, tiled=True)
+
+    gates = [gate_silu[:, j * span : (j + 1) * span] for j in range(chunks)]
+    gathered, returned = [sum_and_gather(parts[0], gates[0])], []
+    up_rows = weights[0]
     for j in range(chunks):
+        if j + 1 < chunks:
+            gathered[j], parts[j + 1] = lax.optimization_barrier((gathered[j], parts[j + 1]))
         grads = (
             lax.dot_general(
                 act_full, gathered[j][:, :span], over_tokens, preferred_element_type=F32
@@ -318,30 +354,34 @@
             ).astype(BF16),
         )
         outgoing = pick_rows(place, grads, block_rows, sections * per_dest)
+        if j + 1 < chunks:
+            gates[j + 1], outgoing = lax.optimization_barrier((gates[j + 1], outgoing))
+            gathered.append(sum_and_gather(parts[j + 1], gates[j + 1]))
+        else:
+            up_rows, outgoing = lax.optimization_barrier((up_rows, outgoing))
+            returned, outgoing = lax.optimization_barrier((returned, outgoing))
         arrivals = lax.all_to_all(outgoing, "section", split_axis=0, concat_axis=0, tiled=True)
         updated = adam_slots(sources, count.reshape(1), fixes, arrivals, states, j, per_dest)
+        if j + 1 < chunks:
+            act_full, cot_full, updated = lax.optimization_barrier((act_full, cot_full, updated))
         returned.append(
             lax.all_to_all(updated, "section", split_axis=0, concat_axis=0, tiled=True)
         )
 
     split = sections // ranks
     back_up = jnp.concatenate([each[:, :span] for each in gathered], axis=1)
-    back_up = back_up.reshape(ranks, tok_dev, hidden_units)
-    up_rows = weights[0].reshape(split, row_count // split, hidden_units)
+    up_rows = up_rows.reshape(split, row_count // split, hidden_units)
     in_part = jnp.stack(
         [
             lax.dot_general(
-                back_up[i // split],
-                up_rows[i % split],
-                (((1,), (1,)), ((), ())),
-                preferred_element_type=F32,
+                back_up, up_rows[h], (((1,), (1,)), ((), ())), preferred_element_type=F32
             ).astype(BF16)
-            for i in range(sections)
+            for h in range(split)
         ]
-    )
+    ).reshape(sections, tok_dev, row_count // split)
     reduced = lax.psum_scatter(in_part, "section", scatter_dimension=0, tiled=True)
     routes = [
-        (s * ranks + k, (split * k + s % split) * ranks + s // split)
+        (s * ranks + k, (split * k + s // ranks) * ranks + s % ranks)
         for s in range(sections)
         for k in range(ranks)
     ]

time: 828 us -> 582 us (0.70)
  Pallas kernels: 409 us -> 125 us
  blocking collectives: 9.46 us -> 149 us
  waiting for transfers between devices: 285 us -> 195 us
  starting transfers between devices: 20.5 us -> 11.6 us
  matrix products: 65.5 us -> 57.2 us
    all_to_all x0 -> x2, blocking collectives: none -> 139 us  [the longest x1 76.3 us: per_device(): lax.all_to_all(updated, 'section', split_axis=0, concat_axis=0, tiled=True)]
    pallas_call x2, Pallas kernels: 131 us -> 6.29 us  [pick_rows(): pl.pallas_call(body, out_shape=jax.ShapeDtypeStruct((slots, rows, cols),...]
    pallas_call x1, Pallas kernels: 129 us -> 5.47 us  [place_rows(): pl.pallas_call(body, out_shape=jax.ShapeDtypeStruct((2, row_blocks * rows...]
    all_to_all x2 -> x1, waiting for transfers between devices: 130 us -> 66.6 us  [per_device(): lax.all_to_all(updated, 'section', split_axis=0, concat_axis=0, tiled=True)]
    pallas_call x1, Pallas kernels: 133 us -> 81.8 us  [spread(): pl.pallas_call(body, out_shape=(out, out), in_specs=[anywhere, anywhere],...]
    all_to_all x2 -> x1, waiting for transfers between devices: 37.3 us -> 18.4 us  [per_device(): lax.all_to_all(outgoing, 'section', split_axis=0, concat_axis=0, tiled=True)]
    pallas_call x2, Pallas kernels: 16.3 us -> 31.8 us  [adam_slots(): pl.pallas_call(adam_kernel, out_shape=jax.ShapeDtypeStruct(arrivals.shape...]
  transfers between devices with their start and end apart: 10 -> 8, of which waited for: 6 -> 6; matrix products, arithmetic and copies ran while one was open for 8% -> 6% of each run, Pallas kernels for 33% -> 7%
where the time goes in v3:
time: 582 us; the launch traced here: 581 us
  waiting for transfers between devices  195 us (34%)
  blocking collectives  149 us (26%)
  Pallas kernels  125 us (21%)
  matrix products  57.2 us (10%)
  other arithmetic  16.5 us (3%)
  between operations  15.9 us (3%)
  starting transfers between devices  11.6 us (2%)
  local copies, waits for them, and re-layouts  11.1 us (2%)
    pallas_call x1, Pallas kernels, spread(): pl.pallas_call(body, out_shape=(out, out), in_specs=[anywhere, anywhere],...  81.8 us
    all_to_all x1, blocking collectives, per_device(): lax.all_to_all(updated, 'section', split_axis=0, concat_axis=0, tiled=True)  76.3 us
    reduce_scatter x2, waiting for transfers between devices, sum_and_gather(): lax.psum_scatter(part, 'dp', scatter_dimension=0, tiled=True).astype(F32)  73.3 us
    all_to_all x1, waiting for transfers between devices, per_device(): lax.all_to_all(updated, 'section', split_axis=0, concat_axis=0, tiled=True)  66.6 us
    all_to_all x1, blocking collectives, per_device(): lax.all_to_all(outgoing, 'section', split_axis=0, concat_axis=0, tiled=True)  62.7 us
    all_gather x2, waiting for transfers between devices, sum_and_gather(): return lax.all_gather(local, 'dp', axis=0, tiled=True)  36.7 us
    pallas_call x2, Pallas kernels, adam_slots(): pl.pallas_call(adam_kernel, out_shape=jax.ShapeDtypeStruct(arrivals.shape...  31.8 us
    all_to_all x1, waiting for transfers between devices, per_device(): lax.all_to_all(outgoing, 'section', split_axis=0, concat_axis=0, tiled=True)  18.4 us
  transfers between devices with their start and end apart: 8, of which 6 were waited for; matrix products, arithmetic and copies ran while one was open for 6% of the time, Pallas kernels for 7%

profile of v3, /device:TPU:0, one launch (start us, length us, event | category | flops | bytes accessed | tf_op | source)
XLA Modules:
  0.0 581.5 jit_solution(5960564748712831983)
XLA Ops:
  7.2 0.8 copy.15
  8.4 1.2 dynamic-slice
  10.3 0.2 dynamic-update-slice
  10.5 9.5 %all-reduce = s32[64]{0:T(128)S(1)} all-reduce(s32[64]{0:T(128)S(1)} %dynamic-update-slice), channel_id=2, replica_groups=mesh['section'=8,'dp'=4] {'section'}, use_global_device_ids=true, to_apply=%add | all-reduce | flops 64 | bytes 512
  20.1 3.8 slice_bitcast_fusion.1
  23.9 81.8 %spread.1 = (bf16[2048,2048]{1,0:T(8,128)(2,1)}, bf16[2048,2048]{1,0:T(8,128)(2,1)}) custom-call(bf16[512,8192]{1,0:T(8,128)(2,1)} %refs_0_, bf16[512,8192]{1,0:T(8,128)(2,1)} %refs_1_), custom_call_target="tpu_custom_call" | custom-call | bytes 134217728 | tf_op jit(solution)/shard_map/spread/pallas_call | solution.py:112
  105.7 6.1 %convolution_convert_fusion.7 = bf16[2048,256]{0,1:T(8,128)(2,1)S(1)} fusion(bf16[2048,2048]{1,0:T(8,128)(2,1)} %get-tuple-element.28, bf16[2048,512]{1,0:T(8,128)(2,1)} %get-tuple-element.36), kind=kOutput, calls=%fused_computation.10 | convolution fusion | flops 2148007936 | bytes 10485760 | tf_op jit(solution)/shard_map/dot_general | solution.py:330
  111.9 2.4 convolution_convert_fusion.6
  114.2 1.5 pad_maximum_fusion.1
  115.8 0.2 copy.16
  116.0 0.3 convert_multiply_fusion
  116.4 50.8 %reduce-scatter.4.cloned.1.call-done = bf16[512,512]{0,1:T(8,128)(2,1)} async-done(((bf16[2048,512]{0,1:T(8,128)(2,1)}), bf16[512,512]{0,1:T(8,128)(2,1)}) %reduce-scatter.4.cloned.1.call-update) | async-done | bytes 524304 | tf_op jit(solution)/shard_map/reduce_scatter | solution.py:338
  167.2 2.0 fusion.8
  169.2 0.2 reduce-scatter.6.cloned.1.call-start
  169.4 6.0 %convolution_convert_fusion.5 = bf16[2048,256]{0,1:T(8,128)(2,1)S(1)} fusion(bf16[2048,2048]{1,0:T(8,128)(2,1)} %get-tuple-element.28, bf16[2048,512]{1,0:T(8,128)(2,1)} %get-tuple-element.36), kind=kOutput, calls=%fused_computation.8 | convolution fusion | flops 2148007936 | bytes 10485760 | tf_op jit(solution)/shard_map/dot_general | solution.py:330
  175.4 6.1 %convolution_convert_fusion.4 = bf16[2048,256]{0,1:T(8,128)(2,1)S(1)} fusion(bf16[2048,2048]{1,0:T(8,128)(2,1)} %get-tuple-element.27, bf16[2048,512]{1,0:T(8,128)(2,1)S(1)} %get-tuple-element.29), kind=kOutput, calls=%fused_computation.7 | convolution fusion | flops 2148007936 | bytes 10485760 | tf_op jit(solution)/shard_map/dot_general | solution.py:331
  181.5 1.4 pad_maximum_fusion.2
  182.9 31.8 %all-gather.4.cloned.1.call-done = bf16[2048,512]{0,1:T(8,128)(2,1)} async-done(((bf16[512,512]{0,1:T(8,128)(2,1)}), bf16[2048,512]{0,1:T(8,128)(2,1)}) %all-gather.4.cloned.1.call-update) | async-done | bytes 2097168 | tf_op jit(solution)/shard_map/all_gather | solution.py:340
  214.8 0.5 multiply_add_fusion.place_ref
  215.3 7.3 %convolution_convert_fusion.3.up_ref = bf16[2048,256]{1,0:T(8,128)(2,1)} fusion(bf16[2048,2048]{1,0:T(8,128)(2,1)} %get-tuple-element.27, bf16[2048,512]{0,1:T(8,128)(2,1)} %all-gather.4.cloned.1.call-done), kind=kOutput, calls=%fused_computation.6 | convolution fusion | flops 2148007936 | bytes 10485760 | tf_op jit(solution)/shard_map/dot_general | solution.py:349
  222.6 6.9 %convolution_convert_fusion.2.down_ref = bf16[2048,256]{1,0:T(8,128)(2,1)} fusion(bf16[2048,2048]{1,0:T(8,128)(2,1)} %get-tuple-element.28, bf16[2048,512]{0,1:T(8,128)(2,1)S(1)} %copy-done.2), kind=kOutput, calls=%fused_computation.5 | convolution fusion | flops 2148007936 | bytes 10485760 | tf_op jit(solution)/shard_map/dot_general | solution.py:352
  229.5 3.1 pick_rows.2
  232.6 4.6 all-to-all-start
  237.2 22.5 %reduce-scatter.6.cloned.1.call-done = bf16[512,512]{0,1:T(8,128)(2,1)} async-done(((bf16[2048,512]{0,1:T(8,128)(2,1)}), bf16[512,512]{0,1:T(8,128)(2,1)}) %reduce-scatter.6.cloned.1.call-update) | async-done | bytes 524304 | tf_op jit(solution)/shard_map/reduce_scatter | solution.py:338
  259.8 2.0 fusion.9
  261.8 0.3 reduce-scatter.8.cloned.1.call-start
  263.1 0.6 fusion.17
  264.3 0.7 pad_maximum_fusion.6.fix_ref
  264.9 0.7 select_reduce_fusion.1.source_ref
  265.7 2.3 slice.56
  268.0 18.4 %all-to-all-done.grad_ref = bf16[64,128,256]{2,1,0:T(8,128)(2,1)} async-done(((bf16[64,128,256]{2,1,0:T(8,128)(2,1)}), bf16[64,128,256]{2,1,0:T(8,128)(2,1)}, u32[]{:S(2)}, u32[]{:S(2)}) %all-to-all-start) | async-done | bytes 4194336 | tf_op jit(solution)/shard_map/all_to_all | solution.py:363
  286.3 15.9 %adam.2 = bf16[64,128,256]{2,1,0:T(8,128)(2,1)} custom-call(s32[6]{0:T(128)} %select_reduce_fusion.1.source_ref, s32[1]{0:T(128)} %bitcast.5.count_ref, f32[2]{0:T(128)} %pad_maximum_fusion.6.fix_ref, bf16[64,128,256]{2,1,0:T(8,128)(2,1)} %all-to-all-done.grad_ref, f32[48,128,512]{2,1,0:T(8,128)} %bitcast.29, f32[48,128,512]{2,1,0:T(8,128)} %bitcast.31, ...), custom_call_target="tpu_custom_call" | custom-call | flops 31457280 | bytes 25165824 | tf_op jit(solution)/shard_map/adam/pallas_call | solution.py:165
  302.3 4.9 all-gather.6.cloned.1.call-done
  307.2 7.3 %convolution_convert_fusion.1.up_ref = bf16[2048,256]{1,0:T(8,128)(2,1)} fusion(bf16[2048,2048]{1,0:T(8,128)(2,1)} %get-tuple-element.27, bf16[2048,512]{0,1:T(8,128)(2,1)} %all-gather.6.cloned.1.call-done), kind=kOutput, calls=%fused_computation.4 | convolution fusion | flops 2148007936 | bytes 10485760 | tf_op jit(solution)/shard_map/dot_general | solution.py:349
  314.5 7.0 %convolution_convert_fusion.down_ref = bf16[2048,256]{1,0:T(8,128)(2,1)} fusion(bf16[2048,2048]{1,0:T(8,128)(2,1)} %get-tuple-element.28, bf16[2048,512]{0,1:T(8,128)(2,1)S(1)} %copy-done.3), kind=kOutput, calls=%fused_computation.3 | convolution fusion | flops 2148007936 | bytes 10485760 | tf_op jit(solution)/shard_map/dot_general | solution.py:352
  321.5 3.2 pick_rows.3
  324.6 1.3 slice.69
  326.0 3.7 convert_bitcast_fusion
  329.7 4.4 convert_bitcast_fusion.1
  334.2 6.2 %pad_maximum_fusion = bf16[2,2048,1024]{2,1,0:T(8,128)(2,1)} fusion(bf16[1,2048,1024]{2,1,0:T(8,128)(2,1)S(1)} %convert_bitcast_fusion, bf16[1,2048,1024]{2,1,0:T(8,128)(2,1)} %convert_bitcast_fusion.1), kind=kLoop, calls=%fused_computation | loop fusion | flops 4194304 | bytes 16777216 | tf_op jit(solution)/shard_map/stack | solution.py:374
  340.4 76.3 %all_to_all.20.refs_0_ = bf16[64,128,256]{2,1,0:T(8,128)(2,1)} all-to-all(bf16[64,128,256]{2,1,0:T(8,128)(2,1)} %adam.2), channel_id=1, replica_groups=mesh['section'=8,'dp'=4] {'section'}, dimensions={0} | all-to-all | bytes 8388608 | tf_op jit(solution)/shard_map/all_to_all | solution.py:368
  416.7 62.7 %all_to_all.21.grad_ref = bf16[64,128,256]{2,1,0:T(8,128)(2,1)} all-to-all(bf16[64,128,256]{2,1,0:T(8,128)(2,1)S(1)} %copy-done), channel_id=1, replica_groups=mesh['section'=8,'dp'=4] {'section'}, dimensions={0} | all-to-all | bytes 8388608 | tf_op jit(solution)/shard_map/all_to_all | solution.py:363
  479.5 15.9 %adam.3 = bf16[64,128,256]{2,1,0:T(8,128)(2,1)} custom-call(s32[6]{0:T(128)} %select_reduce_fusion.1.source_ref, s32[1]{0:T(128)} %bitcast.5.count_ref, f32[2]{0:T(128)} %pad_maximum_fusion.6.fix_ref, bf16[64,128,256]{2,1,0:T(8,128)(2,1)} %all_to_all.21.grad_ref, f32[48,128,512]{2,1,0:T(8,128)} %bitcast.30, f32[48,128,512]{2,1,0:T(8,128)} %bitcast.32, ...), custom_call_target="tpu_custom_call" | custom-call | flops 31457280 | bytes 25165824 | tf_op jit(solution)/shard_map/adam/pallas_call | solution.py:165
  495.4 4.6 all-to-all-start.3
  500.0 1.9 collective-permute-start
  501.9 66.6 %all-to-all-done.3.refs_1_ = bf16[64,128,256]{2,1,0:T(8,128)(2,1)} async-done(((bf16[64,128,256]{2,1,0:T(8,128)(2,1)}), bf16[64,128,256]{2,1,0:T(8,128)(2,1)}, u32[]{:S(2)}, u32[]{:S(2)}) %all-to-all-start.3) | async-done | bytes 4194336 | tf_op jit(solution)/shard_map/all_to_all | solution.py:368
  568.5 5.5 place_rows.1
  574.0 1.0 copy.20
  (34 shorter events, 1.1 us)
Async XLA Ops:
  7.2 160.1 %reduce-scatter.4.cloned.1.call-start = ((), (), s32[]{:S(2)}) async-start(), calls=%async_computation.7 | async-start | bytes 2621440 | tf_op jit(solution)/shard_map/reduce_scatter | solution.py:338
  105.7 6.2 %copy-start.5 = (bf16[2048,2048]{1,0:T(8,128)(2,1)S(1)}, bf16[2048,2048]{1,0:T(8,128)(2,1)}, u32[]{:S(2)}) copy-start(bf16[2048,2048]{1,0:T(8,128)(2,1)} %get-tuple-element.27) | copy-start | bytes 25165828
  114.2 1.6 copy-start.4
  115.8 99.0 %all-gather.4.cloned.1.call-start = ((), (), s32[]{:S(2)}) async-start(), calls=%async_computation.8 | async-start | bytes 2621440 | tf_op jit(solution)/shard_map/all_gather | solution.py:340
  169.2 90.6 %reduce-scatter.6.cloned.1.call-start = ((), (), s32[]{:S(2)}) async-start(), calls=%async_computation.9 | async-start | bytes 2621440 | tf_op jit(solution)/shard_map/reduce_scatter | solution.py:338
  215.3 7.3 %copy-start.2 = (bf16[2048,512]{0,1:T(8,128)(2,1)S(1)}, bf16[2048,512]{0,1:T(8,128)(2,1)}, u32[]{:S(2)}) copy-start(bf16[2048,512]{0,1:T(8,128)(2,1)} %all-gather.4.cloned.1.call-done) | copy-start | bytes 6291460
  232.6 53.7 %all-to-all-start = ((bf16[64,128,256]{2,1,0:T(8,128)(2,1)}), bf16[64,128,256]{2,1,0:T(8,128)(2,1)}, u32[]{:S(2)}, u32[]{:S(2)}) async-start(bf16[64,128,256]{2,1,0:T(8,128)(2,1)} %pick_rows.2), calls=%async_computation.2 | async-start | bytes 8388608 | tf_op jit(solution)/shard_map/all_to_all | solution.py:363
  237.2 70.0 %all-gather.6.cloned.1.call-start = ((), (), s32[]{:S(2)}) async-start(), calls=%async_computation.10 | async-start | bytes 2621440 | tf_op jit(solution)/shard_map/all_gather | solution.py:340
  261.8 238.2 %reduce-scatter.8.cloned.1.call-start = ((), (), s32[]{:S(2)}) async-start(), calls=%async_computation.11 | async-start | bytes 9437184 | tf_op jit(solution)/shard_map/reduce_scatter | solution.py:382
  307.2 7.3 %copy-start.3 = (bf16[2048,512]{0,1:T(8,128)(2,1)S(1)}, bf16[2048,512]{0,1:T(8,128)(2,1)}, u32[]{:S(2)}) copy-start(bf16[2048,512]{0,1:T(8,128)(2,1)} %all-gather.6.cloned.1.call-done) | copy-start | bytes 6291460
  326.0 3.8 copy-start.1
  340.4 76.3 %copy-start = (bf16[64,128,256]{2,1,0:T(8,128)(2,1)S(1)}, bf16[64,128,256]{2,1,0:T(8,128)(2,1)}, u32[]{:S(2)}) copy-start(bf16[64,128,256]{2,1,0:T(8,128)(2,1)} %pick_rows.3) | copy-start | bytes 12582916
  495.4 73.1 %all-to-all-start.3 = ((bf16[64,128,256]{2,1,0:T(8,128)(2,1)}), bf16[64,128,256]{2,1,0:T(8,128)(2,1)}, u32[]{:S(2)}, u32[]{:S(2)}) async-start(bf16[64,128,256]{2,1,0:T(8,128)(2,1)} %adam.3), calls=%async_computation.6 | async-start | bytes 8388608 | tf_op jit(solution)/shard_map/all_to_all | solution.py:368
  500.0 74.0 %collective-permute-start = (bf16[1,512,1024]{2,1,0:T(8,128)(2,1)}, bf16[1,512,1024]{2,1,0:T(8,128)(2,1)S(1)}, u32[]{:S(2)}, u32[]{:S(2)}) collective-permute-start(bf16[1,512,1024]{2,1,0:T(8,128)(2,1)} %reduce-scatter.8.cloned.1.call-done), channel_id=1, source_target_pairs={{0,0},{1,8},{2,16},{3,24},{4,1},{5,9},{6,17},{7,25},{8,2},{9,10},{... | collective-permute-start | bytes 3145736 | tf_op jit(solution)/shard_map/ppermute | solution.py:388
Sparse Core Ops, SparseCore 0:
  115.9 51.2 reduce-scatter.3
  169.4 45.2 all-gather.3
  217.1 42.5 reduce-scatter.5
  261.9 45.2 all-gather.5
  340.5 114.5 reduce-scatter.7
